TPU v7x, 32 devices: a whole 2x2x4 slice. The times are simulated.
32 devices in a mesh: seq: 4 (over x, core), grp: 8 (over z, y).
Axes of the slice: x: 2, y: 2, z: 4, core: 2. Of those that a mesh axis runs over, the one named last changes fastest.
Arguments:
- conv_input: bfloat16 [8, 512, 2688], P('grp', 'seq'), may hold values from -6 to 6
- conv_weight: float32 [4, 2688], replicated, may hold values from -3 to 3
- step_raw: float32 [8, 512, 40], P('grp', 'seq'), may hold values from -9 to 6
- rate_log: float32 [40], replicated, may hold values from -3 to 3.1
- skip_gain: float32 [40], replicated, may hold values from 0.5 to 1.5
- gate_input: bfloat16 [8, 512, 2560], P('grp', 'seq'), may hold values from -6 to 6
- norm_gain: float32 [2560], replicated, may hold values from 0.1 to 1.9
- out_weight: bfloat16 [2560, 2560], P('grp'), may hold values from -0.125 to 0.125
- residual: bfloat16 [8, 512, 2560], P('grp', 'seq'), may hold values from -6 to 6
- moe_gain: float32 [2560], replicated, may hold values from 0.1 to 1.9
- w_gate: bfloat16 [8, 2560, 512], P('grp'), may hold values from -0.125 to 0.125
- w_up: bfloat16 [8, 2560, 512], P('grp'), may hold values from -0.125 to 0.125
- w_down: bfloat16 [8, 512, 2560], P('grp'), may hold values from -0.25 to 0.25
- routes: int32 [8, 512, 2], P('grp', 'seq'), may hold values from 0 to 7, as said below
- route_weights: float32 [8, 512, 2], P('grp', 'seq'), may hold values from 0.2 to 1
Outputs:
- layer_out: bfloat16 [8, 512, 2560], P('grp', 'seq')
Inputs may be any that keep to these rules, and one draw needn't show every extreme that they name: `routes`: within the rows of one device (each aligned block of 128 frames of one manuscript) no expert is named by more than 64 entries, and one expert, the same in every block, is named by exactly 64; the two entries of a frame differ.
All inputs are finite; a program needn't handle non-finite values.
Results may differ from a plain program's by a relative error of at most 0.012.
Values may be sent and summed in bfloat16 or wider, within the bound.
A program may use at most 128 MiB of HBM per device.

v0:
```python
import jax
import jax.numpy as jnp
from jax import lax
from jax.sharding import PartitionSpec as P

EPSILON = 1e-05


def from_behind(value, axis, steps):
    count = lax.axis_size(axis)
    first, last = (max(0, -steps), min(count, count - steps))
    return lax.ppermute(value, axis, [(source, source + steps) for source in range(first, last)])


def on_device(
    conv_input,
    conv_weight,
    step_raw,
    rate_log,
    skip_gain,
    gate_input,
    norm_gain,
    out_weight,
    residual,
    moe_gain,
    w_gate,
    w_up,
    w_down,
    routes,
    route_weights,
):
    highest = lax.Precision.HIGHEST
    frames_in = conv_input[0]
    row_count = frames_in.shape[0]
    tap_count = conv_weight.shape[0]
    channel_count = conv_weight.shape[1]
    head_count = rate_log.shape[0]
    inner_width = gate_input.shape[2]
    head_width = inner_width // head_count
    state_width = (channel_count - inner_width) // 2
    model_width = residual.shape[2]
    edge_rows = frames_in[row_count - (tap_count - 1) :]
    before = from_behind(edge_rows, "seq", 1)
    padded = jnp.concatenate([before, frames_in], axis=0).astype(jnp.float32)
    summed = conv_weight[0][None, :] * padded[0:row_count]
    for offset in range(1, tap_count):
        summed = summed + conv_weight[offset][None, :] * padded[offset : offset + row_count]
    signal = jax.nn.silu(summed).astype(jnp.bfloat16)
    x_part = signal[:, :inner_width]
    b_part = signal[:, inner_width : inner_width + state_width]
    c_part = signal[:, inner_width + state_width :]
    step_size = jax.nn.softplus(step_raw[0])
    log_decay = -step_size * jnp.exp(rate_log)[None, :]
    cumulative = jnp.cumsum(log_decay, axis=0)
    x_values = x_part.astype(jnp.float32).reshape(row_count, head_count, head_width)
    b_values = b_part.astype(jnp.float32)
    c_values = c_part.astype(jnp.float32)
    scores = jnp.dot(c_part, b_part.T, preferred_element_type=jnp.float32)
    positions = jnp.arange(row_count)
    causal = positions[:, None] >= positions[None, :]
    by_head = cumulative.T
    gap_log = by_head[:, :, None] - by_head[:, None, :]
    decay_mask = jnp.where(causal[None], jnp.exp(jnp.where(causal[None], gap_log, 0.0)), 0.0)
    mixing = scores[None] * decay_mask * step_size.T[:, None, :]
    within = jnp.einsum("hts,shp->thp", mixing, x_values, precision=highest)
    tail_weight = jnp.exp(cumulative[-1][None, :] - cumulative) * step_size
    local_state = jnp.einsum(
        "shp,sn->hpn", x_values * tail_weight[:, :, None], b_values, precision=highest
    )
    through = jnp.exp(cumulative[-1])
    entering = jnp.zeros_like(local_state)
    for repeat in range(lax.axis_size("seq") - 1):
        entering = from_behind(through[:, None, None] * entering + local_state, "seq", 1)
    carried = (
        jnp.einsum("tn,hpn->thp", c_values, entering, precision=highest)
        * jnp.exp(cumulative)[:, :, None]
    )
    ssd_out = (within + carried + skip_gain[None, :, None] * x_values).reshape(
        row_count, inner_width
    )
    gated_out = ssd_out * jax.nn.silu(gate_input[0].astype(jnp.float32))
    mean_square = jnp.mean(gated_out * gated_out, axis=1, keepdims=True)
    normed = (gated_out * lax.rsqrt(mean_square + EPSILON) * norm_gain[None, :]).astype(
        jnp.bfloat16
    )
    projected = jnp.dot(
        normed,
        lax.all_gather(out_weight, "grp", axis=0, tiled=True),
        preferred_element_type=jnp.float32,
    )
    mixed_out = (residual[0].astype(jnp.float32) + projected).astype(jnp.bfloat16)
    mixed_float = mixed_out.astype(jnp.float32)
    mixed_square = jnp.mean(mixed_float * mixed_float, axis=1, keepdims=True)
    moe_in = (mixed_float * lax.rsqrt(mixed_square + EPSILON) * moe_gain[None, :]).astype(
        jnp.bfloat16
    )
    experts = lax.axis_size("grp")
    capacity = 4 * row_count // experts
    flat_picks = routes[0].reshape(-1)
    member = (flat_picks[:, None] == jnp.arange(experts)[None, :]).astype(jnp.int32)
    position = jnp.cumsum(member, axis=0) - member
    slot_index = jnp.sum(position * member, axis=1)
    target = (flat_picks * capacity + slot_index).reshape(row_count, 2)
    selector = jnp.any(
        target[None, :, :] == jnp.arange(experts * capacity)[:, None, None], axis=2
    ).astype(jnp.bfloat16)
    outgoing = (
        jnp.dot(selector, moe_in, preferred_element_type=jnp.float32)
        .astype(jnp.bfloat16)
        .reshape(experts, capacity, model_width)
    )
    gate_matrix = w_gate[0]
    up_matrix = w_up[0]
    down_matrix = w_down[0]
    arrived = lax.all_to_all(outgoing, "grp", split_axis=0, concat_axis=0, tiled=True)
    flattened_rows = arrived.reshape(-1, model_width)
    gate_part = jnp.dot(flattened_rows, gate_matrix, preferred_element_type=jnp.float32)
    up_part = jnp.dot(flattened_rows, up_matrix, preferred_element_type=jnp.float32)
    expert_hidden = (jax.nn.silu(gate_part) * up_part).astype(jnp.bfloat16)
    result = (
        jnp.dot(expert_hidden, down_matrix, preferred_element_type=jnp.float32)
        .astype(jnp.bfloat16)
        .reshape(arrived.shape)
    )
    returned = lax.all_to_all(result, "grp", split_axis=0, concat_axis=0, tiled=True)
    back_rows = returned.reshape(experts * capacity, model_width)
    first_out = jnp.take(back_rows, target[:, 0], axis=0).astype(jnp.float32)
    second = jnp.take(back_rows, target[:, 1], axis=0).astype(jnp.float32)
    pair_weights = route_weights[0]
    layer_out = mixed_float + pair_weights[:, 0:1] * first_out + pair_weights[:, 1:2] * second
    return layer_out.astype(jnp.bfloat16)[None]


def solution(mesh):
    in_specs = (
        P("grp", "seq", None),
        P(),
        P("grp", "seq", None),
        P(),
        P(),
        P("grp", "seq", None),
        P(),
        P("grp", None),
        P("grp", "seq", None),
        P(),
        P("grp", None, None),
        P("grp", None, None),
        P("grp", None, None),
        P("grp", "seq", None),
        P("grp", "seq", None),
    )
    out_specs = P("grp", "seq", None)
    return jax.shard_map(
        on_device, mesh=mesh, in_specs=in_specs, out_specs=out_specs, check_vma=False
    )
```

profile of v0, /device:TPU:0, one launch (start us, length us, event | category | flops | bytes accessed | tf_op | source)
XLA Modules:
  0.0 358.3 jit_solution(16381784765529841621)
XLA Ops:
  6.5 0.0 copy-start
  6.5 0.0 all-gather.2.cloned.1.call-start
  6.6 0.7 all-gather.2.cloned.1.call-update
  7.3 1.5 slice_bitcast_fusion
  8.8 3.0 collective-permute-start
  11.7 0.1 copy.68
  11.8 0.0 copy-done.20
  11.9 0.2 reduce_window_sum.26
  12.1 0.5 fusion.73
  12.6 0.7 fusion.74
  13.3 0.7 slice_reduce_fusion.5
  14.0 1.4 copy.66
  15.4 0.1 copy.72
  15.5 0.0 collective-permute-done
  15.5 2.0 copy.67
  17.5 1.7 maximum_convert_fusion
  19.2 2.9 multiply_convert_fusion
  22.1 0.0 copy-start.3
  22.1 0.5 copy-done.17
  22.7 2.3 broadcast_add_fusion
  24.9 5.1 %collective-permute-start.1 = (f32[40,64,64]{2,1,0:T(8,128)}, f32[40,64,64]{2,1,0:T(8,128)}, u32[]{:S(2)}, u32[]{:S(2)}) collective-permute-start(f32[40,64,64]{2,1,0:T(8,128)} %get-tuple-element.19), channel_id=1, source_target_pairs={{0,8},{8,16},{16,24},{1,9},{9,17},{17,25},{2,10},{10,18},{18,26},{... | collective-permute-start | bytes 1966088 | tf_op jit(solution)/shard_map/ppermute | solution.py:12
  30.0 0.1 copy.76
  30.1 0.1 eq.44
  30.3 0.1 eq.40
  30.4 1.5 collective-permute-done.1
  31.9 3.0 multiply_add_fusion.1
  34.9 14.8 %collective-permute-start.2 = (f32[40,64,64]{2,1,0:T(8,128)}, f32[40,64,64]{2,1,0:T(8,128)}, u32[]{:S(2)}, u32[]{:S(2)}) collective-permute-start(f32[40,64,64]{2,1,0:T(8,128)} %multiply_add_fusion.1), channel_id=1, source_target_pairs={{0,8},{8,16},{16,24},{1,9},{9,17},{17,25},{2,10},{10,18},{18,26},{... | collective-permute-start | bytes 1966088 | tf_op jit(solution)/shard_map/ppermute | solution.py:12
  49.8 0.6 reduce-window.6
  50.3 0.2 slice_reduce_fusion.6
  50.6 0.1 fusion.67
  50.7 0.8 reduce_sum.33
  51.5 1.5 add_bitcast_fusion
  52.9 0.0 collective-permute-done.2
  52.9 3.0 multiply_add_fusion
  55.9 16.0 %collective-permute-start.3 = (f32[40,64,64]{2,1,0:T(8,128)}, f32[40,64,64]{2,1,0:T(8,128)}, u32[]{:S(2)}, u32[]{:S(2)}) collective-permute-start(f32[40,64,64]{2,1,0:T(8,128)} %multiply_add_fusion), channel_id=1, source_target_pairs={{0,8},{8,16},{16,24},{1,9},{9,17},{17,25},{2,10},{10,18},{18,26},{... | collective-permute-start | bytes 1966088 | tf_op jit(solution)/shard_map/ppermute | solution.py:12
  72.0 0.6 iota_compare_fusion.1
  72.6 0.9 copy.71
  73.5 0.7 copy.69
  74.2 0.1 copy.73
  74.2 2.4 copy.75
  76.6 0.1 copy.79
  76.7 0.1 fusion.53
  76.8 0.2 fusion.62
  77.0 0.0 copy-start.4
  77.0 0.0 copy-start.21
  77.0 4.3 %fusion.14 = f32[128,40,64]{0,2,1:T(8,128)S(1)} fusion(bf16[128,40,64]{0,2,1:T(8,128)(2,1)} %bitcast.124, f32[40,128]{1,0:T(8,128)S(1)} %copy.71, f32[40,128]{1,0:T(8,128)S(1)} %copy-done.12, f32[128,128]{1,0:T(8,128)S(1)} %fusion.62, pred[128,128]{1,0:T(8,128)(4,1)S(1)} %copy-done.13), kind=kOutput, calls=%fused_computation.21 | convolution fusion | flops 506593280 | bytes 2088960 | tf_op jit(solution)/shard_map/hts,shp->thp/dot_general | solution.py:65
  81.4 0.0 collective-permute-done.3
  81.4 3.6 multiply_reduce_fusion.1
  85.0 3.0 copy.74
  88.0 107.2 %all-gather.2.cloned.1.call-done = bf16[2560,2560]{1,0:T(8,128)(2,1)} async-done(((bf16[320,2560]{1,0:T(8,128)(2,1)}), bf16[2560,2560]{1,0:T(8,128)(2,1)}) %all-gather.2.cloned.1.call-update) | async-done | bytes 13107216 | tf_op jit(solution)/shard_map/all_gather | solution.py:88
  195.1 7.3 %multiply_reduce_fusion = (f32[128]{0:T(128)S(1)}, f32[128,2560]{1,0:T(8,128)S(1)}) fusion(bf16[2560,2560]{1,0:T(8,128)(2,1)} %all-gather.2.cloned.1.call-done, f32[128,2560]{1,0:T(8,128)} %copy.74, f32[2560]{0:T(1024)S(1)} %copy-done.19, f32[128]{0:T(128)S(1)} %add_rsqrt_fusion.1, bf16[1,128,2560]{2,1,0:T(8,128)(2,1)S(1)} %copy-done.6, ...), kind=kOutput, calls=%fused_computation.46 | convolution fusion | flops 1682636672 | bytes 17050624 | tf_op jit(solution)/shard_map/dot_general | solution.py:86
  202.5 0.9 convolution_convert_fusion.1
  203.4 0.1 copy-done.1
  203.6 62.4 %all_to_all.10 = bf16[8,64,2560]{2,1,0:T(8,128)(2,1)S(1)} all-to-all(bf16[8,64,2560]{2,1,0:T(8,128)(2,1)S(1)} %bitcast.118), channel_id=1, replica_groups=mesh['seq'=4,'grp'=8] {'grp'}, dimensions={0} | all-to-all | bytes 5242880 | tf_op jit(solution)/shard_map/all_to_all | solution.py:115
  266.0 1.5 copy-done.2
  267.5 2.5 fusion.5
  270.0 7.2 %convolution_convert_fusion = bf16[512,2560]{1,0:T(8,128)(2,1)} fusion(bf16[1,512,2560]{2,1,0:T(8,128)(2,1)S(1)} %copy-done, bf16[512,2560]{1,0:T(8,128)(2,1)} %bitcast.122, bf16[1,2560,512]{2,1,0:T(8,128)(2,1)} %param.28, f32[512,512]{1,0:T(8,128)} %fusion.5), kind=kOutput, calls=%fused_computation.2 | convolution fusion | flops 2687238144 | bytes 11534336 | tf_op jit(solution)/shard_map/dot_general | solution.py:121
  277.3 4.5 %all-to-all-start.1 = ((bf16[8,64,2560]{2,1,0:T(8,128)(2,1)}), bf16[8,64,2560]{2,1,0:T(8,128)(2,1)}, u32[]{:S(2)}, u32[]{:S(2)}) async-start(bf16[8,64,2560]{2,1,0:T(8,128)(2,1)} %bitcast.120), calls=%async_computation.1 | async-start | bytes 5242880 | tf_op jit(solution)/shard_map/all_to_all | solution.py:125
  281.8 0.1 reduce_sum.35
  282.0 0.2 slice_reduce_fusion.1
  282.2 58.2 %all-to-all-done.1 = bf16[8,64,2560]{2,1,0:T(8,128)(2,1)} async-done(((bf16[8,64,2560]{2,1,0:T(8,128)(2,1)}), bf16[8,64,2560]{2,1,0:T(8,128)(2,1)}, u32[]{:S(2)}, u32[]{:S(2)}) %all-to-all-start.1) | async-done | bytes 2621472 | tf_op jit(solution)/shard_map/all_to_all | solution.py:125
  340.4 3.7 %gather_fusion = bf16[128,2560]{1,0:T(8,128)(2,1)S(1)} fusion(bf16[512,2560]{1,0:T(8,128)(2,1)} %bitcast.26, s32[1024]{0:T(1024)S(1)} %pad_clamp_fusion.1), kind=kCustom, calls=%fused_computation.clone | custom fusion | bytes 1311232 | tf_op jit(solution)/shard_map/jit(_take)/gather | solution.py:127
  344.1 4.5 %gather_fusion.1 = bf16[128,2560]{1,0:T(8,128)(2,1)} fusion(bf16[512,2560]{1,0:T(8,128)(2,1)} %bitcast.26, s32[1024]{0:T(1024)S(1)} %pad_clamp_fusion), kind=kCustom, calls=%fused_computation.1.clone | custom fusion | bytes 1311232 | tf_op jit(solution)/shard_map/jit(_take)/gather | solution.py:128
  348.7 2.8 fusion.43
  (51 shorter events, 0.3 us)
Async XLA Ops:
  6.5 263.5 %copy-start = (bf16[1,512,2560]{2,1,0:T(8,128)(2,1)S(1)}, bf16[1,512,2560]{2,1,0:T(8,128)(2,1)}, u32[]{:S(2)}) copy-start(bf16[1,512,2560]{2,1,0:T(8,128)(2,1)} %param.29) | copy-start | bytes 7864324
  6.5 5.2 %copy-start.11 = (f32[1,128,40]{1,2,0:T(8,128)S(1)}, f32[1,128,40]{1,2,0:T(8,128)}, u32[]{:S(2)}) copy-start(f32[1,128,40]{1,2,0:T(8,128)} %param.19) | copy-start | bytes 61444
  6.5 5.3 %copy-start.20 = (f32[40]{0:T(128)S(1)}, f32[40]{0:T(128)}, u32[]{:S(2)}) copy-start(f32[40]{0:T(128)} %param.20) | copy-start | bytes 484
  6.5 6.7 %copy-start.10 = (f32[4,2688]{1,0:T(4,128)S(1)}, f32[4,2688]{1,0:T(4,128)}, u32[]{:S(2)}) copy-start(f32[4,2688]{1,0:T(4,128)} %param.18) | copy-start | bytes 129028
  6.5 188.6 %all-gather.2.cloned.1.call-start = ((), (), s32[]{:S(2)}) async-start(), calls=%async_computation.2 | async-start | bytes 14745600 | tf_op jit(solution)/shard_map/all_gather | solution.py:88
  8.8 6.7 %collective-permute-start = (bf16[3,2688]{1,0:T(4,128)(2,1)}, bf16[3,2688]{1,0:T(4,128)(2,1)}, u32[]{:S(2)}, u32[]{:S(2)}) collective-permute-start(bf16[3,2688]{1,0:T(4,128)(2,1)} %slice_bitcast_fusion), channel_id=1, source_target_pairs={{0,8},{8,16},{16,24},{1,9},{9,17},{17,25},{2,10},{10,18},{18,26},{... | collective-permute-start | bytes 48392 | tf_op jit(solution)/shard_map/ppermute | solution.py:12
  17.5 1.7 copy-start.8
  17.5 1.7 copy-start.9
  22.1 0.6 copy-start.17
  22.1 2.8 copy-start.3
  22.7 7.3 %copy-start.15 = (s32[1,128,2]{1,2,0:T(2,128)S(1)}, s32[1,128,2]{1,2,0:T(2,128)}, u32[]{:S(2)}) copy-start(s32[1,128,2]{1,2,0:T(2,128)} %param.30) | copy-start | bytes 3076
  24.9 7.0 %collective-permute-start.1 = (f32[40,64,64]{2,1,0:T(8,128)}, f32[40,64,64]{2,1,0:T(8,128)}, u32[]{:S(2)}, u32[]{:S(2)}) collective-permute-start(f32[40,64,64]{2,1,0:T(8,128)} %get-tuple-element.19), channel_id=1, source_target_pairs={{0,8},{8,16},{16,24},{1,9},{9,17},{17,25},{2,10},{10,18},{18,26},{... | collective-permute-start | bytes 1966088 | tf_op jit(solution)/shard_map/ppermute | solution.py:12
  34.9 18.0 %collective-permute-start.2 = (f32[40,64,64]{2,1,0:T(8,128)}, f32[40,64,64]{2,1,0:T(8,128)}, u32[]{:S(2)}, u32[]{:S(2)}) collective-permute-start(f32[40,64,64]{2,1,0:T(8,128)} %multiply_add_fusion.1), channel_id=1, source_target_pairs={{0,8},{8,16},{16,24},{1,9},{9,17},{17,25},{2,10},{10,18},{18,26},{... | collective-permute-start | bytes 1966088 | tf_op jit(solution)/shard_map/ppermute | solution.py:12
  55.9 25.5 %collective-permute-start.3 = (f32[40,64,64]{2,1,0:T(8,128)}, f32[40,64,64]{2,1,0:T(8,128)}, u32[]{:S(2)}, u32[]{:S(2)}) collective-permute-start(f32[40,64,64]{2,1,0:T(8,128)} %multiply_add_fusion), channel_id=1, source_target_pairs={{0,8},{8,16},{16,24},{1,9},{9,17},{17,25},{2,10},{10,18},{18,26},{... | collective-permute-start | bytes 1966088 | tf_op jit(solution)/shard_map/ppermute | solution.py:12
  74.2 2.5 copy-start.7
  74.2 2.8 copy-start.12
  74.2 2.8 copy-start.13
  77.0 4.4 %copy-start.4 = (bf16[128,2560]{0,1:T(8,128)(2,1)S(1)}, bf16[128,2560]{0,1:T(8,128)(2,1)}, u32[]{:S(2)}) copy-start(bf16[128,2560]{0,1:T(8,128)(2,1)} %copy-done.3) | copy-start | bytes 1966084
  77.0 4.4 %copy-start.5 = (f32[1,128,2560]{1,2,0:T(8,128)S(1)}, f32[1,128,2560]{1,2,0:T(8,128)}, u32[]{:S(2)}) copy-start(f32[1,128,2560]{1,2,0:T(8,128)} %copy.75) | copy-start | bytes 3932164
  77.0 4.4 %copy-start.21 = (f32[40]{0:T(128)S(1)}, f32[40]{0:T(128)}, u32[]{:S(2)}) copy-start(f32[40]{0:T(128)} %param.21) | copy-start | bytes 484
  85.0 110.2 %copy-start.6 = (bf16[1,128,2560]{2,1,0:T(8,128)(2,1)S(1)}, bf16[1,128,2560]{2,1,0:T(8,128)(2,1)}, u32[]{:S(2)}) copy-start(bf16[1,128,2560]{2,1,0:T(8,128)(2,1)} %param.22) | copy-start | bytes 1966084
  85.0 110.2 %copy-start.19 = (f32[2560]{0:T(1024)S(1)}, f32[2560]{0:T(1024)}, u32[]{:S(2)}) copy-start(f32[2560]{0:T(1024)} %param.23) | copy-start | bytes 30724
  88.0 114.5 %copy-start.14 = (f32[2560]{0:T(1024)S(1)}, f32[2560]{0:T(1024)}, u32[]{:S(2)}) copy-start(f32[2560]{0:T(1024)} %param.26) | copy-start | bytes 30724
  202.4 1.1 copy-start.1
  203.5 64.0 %copy-start.18 = (bf16[1,2560,512]{2,1,0:T(8,128)(2,1)S(1)}, bf16[1,2560,512]{2,1,0:T(8,128)(2,1)}, u32[]{:S(2)}) copy-start(bf16[1,2560,512]{2,1,0:T(8,128)(2,1)} %param.27) | copy-start | bytes 7864324
  266.0 1.5 copy-start.2
  277.3 4.9 %copy-start.16 = (f32[1,128,2]{1,2,0:T(2,128)S(1)}, f32[1,128,2]{1,2,0:T(2,128)}, u32[]{:S(2)}) copy-start(f32[1,128,2]{1,2,0:T(2,128)} %param.31) | copy-start | bytes 3076
  277.3 63.1 %all-to-all-start.1 = ((bf16[8,64,2560]{2,1,0:T(8,128)(2,1)}), bf16[8,64,2560]{2,1,0:T(8,128)(2,1)}, u32[]{:S(2)}, u32[]{:S(2)}) async-start(bf16[8,64,2560]{2,1,0:T(8,128)(2,1)} %bitcast.120), calls=%async_computation.1 | async-start | bytes 5242880 | tf_op jit(solution)/shard_map/all_to_all | solution.py:125
Sparse Core Ops, SparseCore 0:
  9.6 185.5 all-gather.1
where the time goes:
time: 359 us; the launch traced here: 358 us
  waiting for transfers between devices  168 us (47%)
  blocking collectives  62.4 us (17%)
  starting transfers between devices  43.5 us (12%)
  matrix products  28.3 us (8%)
  local copies, waits for them, and re-layouts  25.2 us (7%)
  other arithmetic  17.6 us (5%)
  between operations  13.7 us (4%)
    all_gather x1, waiting for transfers between devices, on_device(): lax.all_gather(out_weight, 'grp', axis=0, tiled=True)  107 us
    all_to_all x1, blocking collectives, on_device(): lax.all_to_all(outgoing, 'grp', split_axis=0, concat_axis=0, tiled=True)  62.4 us
    all_to_all x1, waiting for transfers between devices, on_device(): lax.all_to_all(result, 'grp', split_axis=0, concat_axis=0, tiled=True)  58.2 us
    ppermute x4, starting transfers between devices, from_behind(): lax.ppermute(value, axis, [(source, source + steps) for source in range(f...  38.9 us
    dot_general x1, matrix products, on_device(): jnp.dot(normed, lax.all_gather(out_weight, 'grp', axis=0, tiled=True), pr...  7.31 us
    dot_general x1, matrix products, on_device(): jnp.dot(expert_hidden, down_matrix, preferred_element_type=jnp.float32)  7.24 us
  transfers between devices with their start and end apart: 6, of which 3 were waited for; matrix products, arithmetic and copies ran while one was open for 11% of the time, Pallas kernels for 0%

commit v1 on v0

--- a/solution.py
+++ b/solution.py
@@ -29,7 +29,13 @@
     routes,
     route_weights,
 ):
-    highest = lax.Precision.HIGHEST
+    half = jnp.bfloat16
+    ring = lax.axis_size("seq")
+    own = lax.axis_index("seq")
+    share = out_weight.shape[1] // ring
+    weight_share = lax.all_gather(
+        lax.dynamic_slice_in_dim(out_weight, own * share, share, axis=1), "grp", axis=0, tiled=True
+    )
     frames_in = conv_input[0]
     row_count = frames_in.shape[0]
     tap_count = conv_weight.shape[0]
@@ -61,18 +67,25 @@
     by_head = cumulative.T
     gap_log = by_head[:, :, None] - by_head[:, None, :]
     decay_mask = jnp.where(causal[None], jnp.exp(jnp.where(causal[None], gap_log, 0.0)), 0.0)
-    mixing = scores[None] * decay_mask * step_size.T[:, None, :]
-    within = jnp.einsum("hts,shp->thp", mixing, x_values, precision=highest)
+    mixing = (scores[None] * decay_mask * step_size.T[:, None, :]).astype(half)
+    x_heads = x_part.reshape(row_count, head_count, head_width)
     tail_weight = jnp.exp(cumulative[-1][None, :] - cumulative) * step_size
     local_state = jnp.einsum(
-        "shp,sn->hpn", x_values * tail_weight[:, :, None], b_values, precision=highest
-    )
-    through = jnp.exp(cumulative[-1])
-    entering = jnp.zeros_like(local_state)
-    for repeat in range(lax.axis_size("seq") - 1):
-        entering = from_behind(through[:, None, None] * entering + local_state, "seq", 1)
+        "shp,sn->hpn",
+        (x_values * tail_weight[:, :, None]).astype(half),
+        b_part,
+        preferred_element_type=jnp.float32,
+    ).astype(half)
+    totals = lax.all_gather(cumulative[-1], "seq", axis=0)
+    passing = jnp.zeros_like(totals[0])
+    entering = jnp.zeros(local_state.shape, jnp.float32)
+    for shift in range(1, ring):
+        arrived_state = from_behind(local_state, "seq", shift).astype(jnp.float32)
+        entering = entering + jnp.exp(passing)[:, None, None] * arrived_state
+        passing = passing + totals[jnp.maximum(own - shift, 0)]
+    within = jnp.einsum("hts,shp->thp", mixing, x_heads, preferred_element_type=jnp.float32)
     carried = (
-        jnp.einsum("tn,hpn->thp", c_values, entering, precision=highest)
+        jnp.einsum("tn,hpn->thp", c_part, entering.astype(half), preferred_element_type=jnp.float32)
         * jnp.exp(cumulative)[:, :, None]
     )
     ssd_out = (within + carried + skip_gain[None, :, None] * x_values).reshape(
@@ -83,10 +96,10 @@
     normed = (gated_out * lax.rsqrt(mean_square + EPSILON) * norm_gain[None, :]).astype(
         jnp.bfloat16
     )
-    projected = jnp.dot(
-        normed,
-        lax.all_gather(out_weight, "grp", axis=0, tiled=True),
-        preferred_element_type=jnp.float32,
+    all_rows = lax.all_gather(normed, "seq", axis=0, tiled=True)
+    column_share = jnp.dot(all_rows, weight_share, preferred_element_type=jnp.float32).astype(half)
+    projected = lax.all_to_all(column_share, "seq", split_axis=0, concat_axis=1, tiled=True).astype(
+        jnp.float32
     )
     mixed_out = (residual[0].astype(jnp.float32) + projected).astype(jnp.bfloat16)
     mixed_float = mixed_out.astype(jnp.float32)
@@ -124,8 +137,11 @@
     )
     returned = lax.all_to_all(result, "grp", split_axis=0, concat_axis=0, tiled=True)
     back_rows = returned.reshape(experts * capacity, model_width)
-    first_out = jnp.take(back_rows, target[:, 0], axis=0).astype(jnp.float32)
-    second = jnp.take(back_rows, target[:, 1], axis=0).astype(jnp.float32)
+    slots = jnp.arange(experts * capacity)[None, :]
+    first_pick = (target[:, 0:1] == slots).astype(half)
+    second_pick = (target[:, 1:2] == slots).astype(half)
+    first_out = jnp.dot(first_pick, back_rows, preferred_element_type=jnp.float32)
+    second = jnp.dot(second_pick, back_rows, preferred_element_type=jnp.float32)
     pair_weights = route_weights[0]
     layer_out = mixed_float + pair_weights[:, 0:1] * first_out + pair_weights[:, 1:2] * second
     return layer_out.astype(jnp.bfloat16)[None]

time: 359 us -> 338 us (0.942)
  starting transfers between devices: 43.5 us -> 17.8 us
  waiting for transfers between devices: 168 us -> 180 us
  other arithmetic: 17.6 us -> 10.4 us
  blocking collectives: 62.4 us -> 68.3 us
  local copies, waits for them, and re-layouts: 25.2 us -> 20.7 us
    ppermute x4, starting transfers between devices: 38.9 us -> 9.76 us  [from_behind(): lax.ppermute(value, axis, [(source, source + steps) for source in range(f...]
    ppermute x4, waiting for transfers between devices: 1.54 us -> 23.6 us  [from_behind(): lax.ppermute(value, axis, [(source, source + steps) for source in range(f...]
    all_gather x1 -> x2, waiting for transfers between devices: 107 us -> 88.9 us  [the longest x1 64.2 us: on_device(): lax.all_gather(lax.dynamic_slice_in_dim(out_weight, own * share, share, a...]
    all_to_all x0 -> x1, waiting for transfers between devices: none -> 9.41 us  [on_device(): lax.all_to_all(column_share, 'seq', split_axis=0, concat_axis=1, tiled=True)]
    gather x2 -> x0, local copies, waits for them, and re-layouts: 8.24 us -> none  [the longest x1 4.54 us: on_device(): second = jnp.take(back_rows, target[:, 1], axis=0).astype(jnp.float32)]
    add x2 -> x0, other arithmetic: 5.94 us -> none  [on_device(): through[:, None, None] * entering + local_state]
    all_gather x0 -> x1, blocking collectives: none -> 5.69 us  [on_device(): totals = lax.all_gather(cumulative[-1], 'seq', axis=0)]
    dot_general x4 -> x6, matrix products: 17.5 us -> 14.7 us  [the longest x1 5.75 us: on_device(): jnp.dot(all_rows, weight_share, preferred_element_type=jnp.float32)]
  transfers between devices with their start and end apart: 6 -> 8, of which waited for: 3 -> 6; matrix products, arithmetic and copies ran while one was open for 11% -> 5% of each run, Pallas kernels for 0% -> 0%
where the time goes in v1:
time: 338 us; the launch traced here: 337 us
  waiting for transfers between devices  180 us (53%)
  blocking collectives  68.3 us (20%)
  matrix products  25.6 us (8%)
  local copies, waits for them, and re-layouts  20.7 us (6%)
  starting transfers between devices  17.8 us (5%)
  between operations  13.7 us (4%)
  other arithmetic  10.4 us (3%)
    all_gather x1, waiting for transfers between devices, on_device(): lax.all_gather(lax.dynamic_slice_in_dim(out_weight, own * share, share, a...  64.2 us
    all_to_all x1, blocking collectives, on_device(): lax.all_to_all(outgoing, 'grp', split_axis=0, concat_axis=0, tiled=True)  62.7 us
    all_to_all x1, waiting for transfers between devices, on_device(): lax.all_to_all(result, 'grp', split_axis=0, concat_axis=0, tiled=True)  58.2 us
    all_gather x1, waiting for transfers between devices, on_device(): all_rows = lax.all_gather(normed, 'seq', axis=0, tiled=True)  24.7 us
    ppermute x4, waiting for transfers between devices, from_behind(): lax.ppermute(value, axis, [(source, source + steps) for source in range(f...  23.6 us
    ppermute x4, starting transfers between devices, from_behind(): lax.ppermute(value, axis, [(source, source + steps) for source in range(f...  9.76 us
    all_to_all x1, waiting for transfers between devices, on_device(): lax.all_to_all(column_share, 'seq', split_axis=0, concat_axis=1, tiled=True)  9.41 us
    dot_general x1, matrix products, on_device(): jnp.dot(expert_hidden, down_matrix, preferred_element_type=jnp.float32)  7.24 us
  transfers between devices with their start and end apart: 8, of which 6 were waited for; matrix products, arithmetic and copies ran while one was open for 5% of the time, Pallas kernels for 0%

profile of v1, /device:TPU:0, one launch (start us, length us, event | category | flops | bytes accessed | tf_op | source)
XLA Modules:
  0.0 336.8 jit_solution(5236764994432943655)
XLA Ops:
  6.5 1.5 slice_bitcast_fusion
  8.1 2.9 collective-permute-start
  11.0 0.6 iota_compare_fusion.5
  11.6 1.1 slice_reduce_fusion.5
  12.7 0.8 copy.72
  13.5 0.7 exp.65
  14.2 0.2 reduce_window_sum.26
  14.4 0.7 fusion.72
  15.1 5.7 %all-gather = f32[4,1,40]{2,1,0:T(1,128)S(1)} all-gather(f32[1,1,40]{2,1,0:T(1,128)S(1)} %get-tuple-element.13), channel_id=1, replica_groups=mesh['seq'=4,'grp'=8] {'seq'}, dimensions={0}, use_global_device_ids=true | all-gather | bytes 800 | tf_op jit(solution)/shard_map/all_gather | solution.py:79
  20.8 0.5 exponential_bitcast_fusion
  21.3 1.4 copy.70
  22.8 1.5 copy.75
  24.3 0.7 copy.73
  25.0 0.1 copy.76
  25.0 0.1 copy.77
  25.1 2.4 copy.79
  27.5 1.9 copy.71
  29.5 1.6 maximum_convert_fusion
  31.1 2.9 multiply_convert_fusion.1
  34.1 0.3 convolution_convert_fusion.3
  34.4 2.2 collective-permute-start.1
  36.6 3.3 collective-permute-start.2
  39.9 1.3 collective-permute-start.3
  41.3 0.2 fusion.58
  41.5 0.0 copy-start.15
  41.5 1.1 convolution_bitcast_fusion
  42.6 12.4 %collective-permute-done.2 = bf16[40,64,64]{2,1,0:T(8,128)(2,1)S(1)} collective-permute-done((bf16[40,64,64]{2,1,0:T(8,128)(2,1)S(1)}, bf16[40,64,64]{2,1,0:T(8,128)(2,1)S(1)}, u32[]{:S(2)}, u32[]{:S(2)}) %collective-permute-start.2) | collective-permute-done | bytes 327712 | tf_op jit(solution)/shard_map/ppermute | solution.py:12
  55.0 11.2 %collective-permute-done.3 = bf16[40,64,64]{2,1,0:T(8,128)(2,1)S(1)} collective-permute-done((bf16[40,64,64]{2,1,0:T(8,128)(2,1)S(1)}, bf16[40,64,64]{2,1,0:T(8,128)(2,1)S(1)}, u32[]{:S(2)}, u32[]{:S(2)}) %collective-permute-start.3) | collective-permute-done | bytes 327712 | tf_op jit(solution)/shard_map/ppermute | solution.py:12
  66.3 2.0 multiply_reduce_fusion
  68.3 2.9 copy.78
  71.1 2.6 fusion.33
  73.8 0.0 all-gather.4.cloned.1.call-update
  73.8 0.0 all-gather.6.cloned.1.call-start
  73.8 1.8 constant_dynamic-slice_fusion
  75.7 0.0 all-gather.6.cloned.1.call-update
  75.7 0.1 copy.81
  75.8 0.1 eq.74
  76.0 0.6 reduce-window.6
  76.5 24.7 %all-gather.4.cloned.1.call-done = bf16[512,2560]{1,0:T(8,128)(2,1)} async-done(((bf16[128,2560]{1,0:T(8,128)(2,1)}), bf16[512,2560]{1,0:T(8,128)(2,1)}) %all-gather.4.cloned.1.call-update) | async-done | bytes 2621456 | tf_op jit(solution)/shard_map/all_gather | solution.py:99
  101.2 64.2 %all-gather.6.cloned.1.call-done = bf16[2560,640]{1,0:T(8,128)(2,1)} async-done(((bf16[320,640]{1,0:T(8,128)(2,1)}), bf16[2560,640]{1,0:T(8,128)(2,1)}) %all-gather.6.cloned.1.call-update) | async-done | bytes 3276816 | tf_op jit(solution)/shard_map/all_gather | solution.py:36
  165.4 5.7 %convolution_convert_fusion.2 = bf16[512,640]{1,0:T(8,128)(2,1)} fusion(bf16[512,2560]{1,0:T(8,128)(2,1)} %all-gather.4.cloned.1.call-done, bf16[2560,640]{1,0:T(8,128)(2,1)} %all-gather.6.cloned.1.call-done), kind=kOutput, calls=%fused_computation.32 | convolution fusion | flops 1678049280 | bytes 6553600 | tf_op jit(solution)/shard_map/dot_general | solution.py:100
  171.2 3.5 %all-to-all-start = ((bf16[4,128,640]{2,1,0:T(8,128)(2,1)}), bf16[4,128,640]{2,1,0:T(8,128)(2,1)S(1)}, u32[]{:S(2)}, u32[]{:S(2)}) async-start(bf16[4,128,640]{2,1,0:T(8,128)(2,1)} %bitcast.134), calls=%async_computation | async-start | bytes 1310720 | tf_op jit(solution)/shard_map/all_to_all | solution.py:101
  174.7 0.2 slice_reduce_fusion.6
  174.9 0.1 eq.70
  175.1 0.1 fusion.63
  175.1 0.1 reduce_sum.34
  175.3 0.1 copy.84
  175.4 0.1 fusion.48
  175.5 9.4 %all-to-all-done = bf16[4,128,640]{2,1,0:T(8,128)(2,1)S(1)} async-done(((bf16[4,128,640]{2,1,0:T(8,128)(2,1)}), bf16[4,128,640]{2,1,0:T(8,128)(2,1)S(1)}, u32[]{:S(2)}, u32[]{:S(2)}) %all-to-all-start) | async-done | bytes 655392 | tf_op jit(solution)/shard_map/all_to_all | solution.py:101
  184.9 0.1 convert_bitcast_fusion
  185.0 0.1 copy.85
  185.1 0.9 copy-done.4
  186.1 0.3 fusion.18
  186.4 0.9 convolution_convert_fusion.1
  187.3 62.7 %all_to_all.23 = bf16[8,64,2560]{2,1,0:T(8,128)(2,1)S(1)} all-to-all(bf16[8,64,2560]{2,1,0:T(8,128)(2,1)S(1)} %bitcast.123), channel_id=1, replica_groups=mesh['seq'=4,'grp'=8] {'grp'}, dimensions={0} | all-to-all | bytes 5242880 | tf_op jit(solution)/shard_map/all_to_all | solution.py:128
  250.0 1.5 copy-done.1
  251.5 2.5 fusion.7
  254.1 7.2 %convolution_convert_fusion = bf16[512,2560]{1,0:T(8,128)(2,1)} fusion(bf16[1,512,2560]{2,1,0:T(8,128)(2,1)S(1)} %copy-done, bf16[512,2560]{1,0:T(8,128)(2,1)} %bitcast.128, bf16[1,2560,512]{2,1,0:T(8,128)(2,1)} %param.26, f32[512,512]{1,0:T(8,128)} %fusion.7), kind=kOutput, calls=%fused_computation | convolution fusion | flops 2687238144 | bytes 11534336 | tf_op jit(solution)/shard_map/dot_general | solution.py:134
  261.3 4.5 %all-to-all-start.2 = ((bf16[8,64,2560]{2,1,0:T(8,128)(2,1)}), bf16[8,64,2560]{2,1,0:T(8,128)(2,1)}, u32[]{:S(2)}, u32[]{:S(2)}) async-start(bf16[8,64,2560]{2,1,0:T(8,128)(2,1)} %bitcast.126), calls=%async_computation.2 | async-start | bytes 5242880 | tf_op jit(solution)/shard_map/all_to_all | solution.py:138
  265.8 0.1 reduce_sum.33
  266.0 0.2 slice_reduce_fusion.1
  266.2 58.2 %all-to-all-done.2 = bf16[8,64,2560]{2,1,0:T(8,128)(2,1)} async-done(((bf16[8,64,2560]{2,1,0:T(8,128)(2,1)}), bf16[8,64,2560]{2,1,0:T(8,128)(2,1)}, u32[]{:S(2)}, u32[]{:S(2)}) %all-to-all-start.2) | async-done | bytes 2621472 | tf_op jit(solution)/shard_map/all_to_all | solution.py:138
  324.4 2.3 convolution_multiply_fusion
  326.7 3.2 fusion.3
  (43 shorter events, 0.3 us)
Async XLA Ops:
  6.5 247.5 %copy-start = (bf16[1,512,2560]{2,1,0:T(8,128)(2,1)S(1)}, bf16[1,512,2560]{2,1,0:T(8,128)(2,1)}, u32[]{:S(2)}) copy-start(bf16[1,512,2560]{2,1,0:T(8,128)(2,1)} %param.27) | copy-start | bytes 7864324
  6.5 94.7 %all-gather.4.cloned.1.call-start = ((), (), s32[]{:S(2)}) async-start(), calls=%async_computation.3 | async-start | bytes 3276800 | tf_op jit(solution)/shard_map/all_gather | solution.py:99
  8.1 19.4 %collective-permute-start = (bf16[3,2688]{1,0:T(4,128)(2,1)}, bf16[3,2688]{1,0:T(4,128)(2,1)}, u32[]{:S(2)}, u32[]{:S(2)}) collective-permute-start(bf16[3,2688]{1,0:T(4,128)(2,1)} %slice_bitcast_fusion), channel_id=1, source_target_pairs={{0,8},{8,16},{16,24},{1,9},{9,17},{17,25},{2,10},{10,18},{18,26},{... | collective-permute-start | bytes 48392 | tf_op jit(solution)/shard_map/ppermute | solution.py:12
  34.0 7.4 %copy-start.5 = (f32[40,128]{1,0:T(8,128)S(1)}, f32[40,128]{1,0:T(8,128)}, u32[]{:S(2)}) copy-start(f32[40,128]{1,0:T(8,128)} %copy.75) | copy-start | bytes 61444
  34.0 7.4 %copy-start.6 = (f32[40,128]{1,0:T(8,128)S(1)}, f32[40,128]{1,0:T(8,128)}, u32[]{:S(2)}) copy-start(f32[40,128]{1,0:T(8,128)} %copy.73) | copy-start | bytes 61444
  34.0 7.4 %copy-start.7 = (pred[128,128]{1,0:T(8,128)(4,1)S(1)}, pred[128,128]{1,0:T(8,128)(4,1)}, u32[]{:S(2)}) copy-start(pred[128,128]{1,0:T(8,128)(4,1)} %iota_compare_fusion.5) | copy-start | bytes 49156
  34.4 8.2 %collective-permute-start.1 = (bf16[40,64,64]{2,1,0:T(8,128)(2,1)S(1)}, bf16[40,64,64]{2,1,0:T(8,128)(2,1)S(1)}, u32[]{:S(2)}, u32[]{:S(2)}) collective-permute-start(bf16[40,64,64]{2,1,0:T(8,128)(2,1)S(1)} %convolution_convert_fusion.3), channel_id=1, source_target_pairs={{0,8},{8,16},{16,24},{1,9},{9,17},{17,25},{2,10},{10,18},{18,26},{... | collective-permute-start | bytes 983048 | tf_op jit(solution)/shard_map/ppermute | solution.py:12
  36.6 18.5 %collective-permute-start.2 = (bf16[40,64,64]{2,1,0:T(8,128)(2,1)S(1)}, bf16[40,64,64]{2,1,0:T(8,128)(2,1)S(1)}, u32[]{:S(2)}, u32[]{:S(2)}) collective-permute-start(bf16[40,64,64]{2,1,0:T(8,128)(2,1)S(1)} %convolution_convert_fusion.3), channel_id=1, source_target_pairs={{0,16},{8,24},{1,17},{9,25},{2,18},{10,26},{3,19},{11,27},{4,20},{... | collective-permute-start | bytes 983048 | tf_op jit(solution)/shard_map/ppermute | solution.py:12
  39.9 26.3 %collective-permute-start.3 = (bf16[40,64,64]{2,1,0:T(8,128)(2,1)S(1)}, bf16[40,64,64]{2,1,0:T(8,128)(2,1)S(1)}, u32[]{:S(2)}, u32[]{:S(2)}) collective-permute-start(bf16[40,64,64]{2,1,0:T(8,128)(2,1)S(1)} %convolution_convert_fusion.3), channel_id=1, source_target_pairs={{0,24},{1,25},{2,26},{3,27},{4,28},{5,29},{6,30},{7,31}} | collective-permute-start | bytes 983048 | tf_op jit(solution)/shard_map/ppermute | solution.py:12
  41.5 24.8 %copy-start.3 = (f32[1,128,2560]{1,2,0:T(8,128)S(1)}, f32[1,128,2560]{1,2,0:T(8,128)}, u32[]{:S(2)}) copy-start(f32[1,128,2560]{1,2,0:T(8,128)} %copy.79) | copy-start | bytes 3932164
  41.5 24.8 %copy-start.12 = (f32[40]{0:T(128)S(1)}, f32[40]{0:T(128)}, u32[]{:S(2)}) copy-start(f32[40]{0:T(128)} %get-tuple-element.18) | copy-start | bytes 484
  41.5 24.8 %copy-start.13 = (f32[40]{0:T(128)S(1)}, f32[40]{0:T(128)}, u32[]{:S(2)}) copy-start(f32[40]{0:T(128)} %get-tuple-element.19) | copy-start | bytes 484
  41.5 24.7 %copy-start.15 = (f32[40]{0:T(128)S(1)}, f32[40]{0:T(128)}, u32[]{:S(2)}) copy-start(f32[40]{0:T(128)} %param.19) | copy-start | bytes 484
  68.3 2.9 copy-start.2
  68.3 2.9 copy-start.8
  73.8 1.9 copy-start.10
  73.8 91.6 %all-gather.6.cloned.1.call-start = ((), (), s32[]{:S(2)}) async-start(), calls=%async_computation.4 | async-start | bytes 3686400 | tf_op jit(solution)/shard_map/all_gather | solution.py:36
  171.2 13.7 %all-to-all-start = ((bf16[4,128,640]{2,1,0:T(8,128)(2,1)}), bf16[4,128,640]{2,1,0:T(8,128)(2,1)S(1)}, u32[]{:S(2)}, u32[]{:S(2)}) async-start(bf16[4,128,640]{2,1,0:T(8,128)(2,1)} %bitcast.134), calls=%async_computation | async-start | bytes 1310720 | tf_op jit(solution)/shard_map/all_to_all | solution.py:101
  185.0 1.1 copy-start.4
  185.1 1.2 copy-start.9
  187.3 64.2 %copy-start.14 = (bf16[1,2560,512]{2,1,0:T(8,128)(2,1)S(1)}, bf16[1,2560,512]{2,1,0:T(8,128)(2,1)}, u32[]{:S(2)}) copy-start(bf16[1,2560,512]{2,1,0:T(8,128)(2,1)} %param.25) | copy-start | bytes 7864324
  250.0 1.5 copy-start.1
  261.3 4.9 %copy-start.11 = (f32[1,128,2]{1,2,0:T(2,128)S(1)}, f32[1,128,2]{1,2,0:T(2,128)}, u32[]{:S(2)}) copy-start(f32[1,128,2]{1,2,0:T(2,128)} %param.29) | copy-start | bytes 3076
  261.3 63.1 %all-to-all-start.2 = ((bf16[8,64,2560]{2,1,0:T(8,128)(2,1)}), bf16[8,64,2560]{2,1,0:T(8,128)(2,1)}, u32[]{:S(2)}, u32[]{:S(2)}) async-start(bf16[8,64,2560]{2,1,0:T(8,128)(2,1)} %bitcast.126), calls=%async_computation.2 | async-start | bytes 5242880 | tf_op jit(solution)/shard_map/all_to_all | solution.py:138
Sparse Core Ops, SparseCore 0:
  73.9 27.2 all-gather.3
  103.4 61.9 all-gather.5

commit v2 on v1

--- a/solution.py
+++ b/solution.py
@@ -1,6 +1,10 @@
+import functools
+
 import jax
 import jax.numpy as jnp
 from jax import lax
+from jax.experimental import pallas as pl
+from jax.experimental.pallas import tpu as pltpu
 from jax.sharding import PartitionSpec as P
 
 EPSILON = 1e-05
@@ -10,6 +14,240 @@
     count = lax.axis_size(axis)
     first, last = (max(0, -steps), min(count, count - steps))
     return lax.ppermute(value, axis, [(source, source + steps) for source in range(first, last)])
+
+
+def exchange_kernel(
+    ring,
+    experts,
+    normed_ref,
+    weight_hbm,
+    residual_ref,
+    gain_ref,
+    gate_hbm,
+    up_hbm,
+    down_hbm,
+    send_pick_ref,
+    first_pick_ref,
+    second_pick_ref,
+    pair_ref,
+    out_ref,
+    weight_ref,
+    gate_ref,
+    up_ref,
+    down_ref,
+    rows_in,
+    share_out,
+    share_in,
+    mixed_ref,
+    moe_ref,
+    outgoing,
+    arrived,
+    result,
+    returned,
+    local_sem,
+    rows_send,
+    rows_recv,
+    share_send,
+    share_recv,
+    out_send,
+    out_recv,
+    back_send,
+    back_recv,
+):
+    me = lax.axis_index("seq")
+    mine = lax.axis_index("grp")
+    width = moe_ref.shape[1]
+    stretch = 512 if width % 512 == 0 else 128
+    share = weight_ref.shape[1]
+    capacity = outgoing.shape[1]
+    half = jnp.bfloat16
+    full = jnp.float32
+
+    locals_ = [
+        pltpu.make_async_copy(source, target, local_sem.at[index])
+        for index, (source, target) in enumerate(
+            ((weight_hbm, weight_ref), (gate_hbm, gate_ref), (up_hbm, up_ref), (down_hbm, down_ref))
+        )
+    ]
+    for copy in locals_:
+        copy.start()
+
+    barrier = pltpu.get_barrier_semaphore()
+
+    def greet(axis, own, count):
+        def step(shift, carry):
+            pl.semaphore_signal(
+                barrier,
+                inc=1,
+                device_id={axis: lax.rem(own + shift, count)},
+                device_id_type=pl.DeviceIdType.MESH,
+            )
+            return carry
+
+        lax.fori_loop(1, count, step, 0)
+
+    greet("seq", me, ring)
+    greet("grp", mine, experts)
+    pl.semaphore_wait(barrier, ring - 1 + experts - 1)
+
+    def rows_copy(shift):
+        return pltpu.make_async_remote_copy(
+            src_ref=normed_ref,
+            dst_ref=rows_in.at[shift],
+            send_sem=rows_send.at[shift],
+            recv_sem=rows_recv.at[shift],
+            device_id={"seq": lax.rem(me + shift, ring)},
+            device_id_type=pl.DeviceIdType.MESH,
+        )
+
+    def share_copy(shift):
+        return pltpu.make_async_remote_copy(
+            src_ref=share_out.at[shift],
+            dst_ref=share_in.at[shift],
+            send_sem=share_send.at[shift],
+            recv_sem=share_recv.at[shift],
+            device_id={"seq": lax.rem(me + ring - shift, ring)},
+            device_id_type=pl.DeviceIdType.MESH,
+        )
+
+    def out_copy(shift):
+        return pltpu.make_async_remote_copy(
+            src_ref=outgoing.at[shift],
+            dst_ref=arrived.at[shift],
+            send_sem=out_send.at[shift],
+            recv_sem=out_recv.at[shift],
+            device_id={"grp": lax.rem(mine + shift, experts)},
+            device_id_type=pl.DeviceIdType.MESH,
+        )
+
+    def back_copy(shift):
+        return pltpu.make_async_remote_copy(
+            src_ref=result.at[shift],
+            dst_ref=returned.at[shift],
+            send_sem=back_send.at[shift],
+            recv_sem=back_recv.at[shift],
+            device_id={"grp": lax.rem(mine + experts - shift, experts)},
+            device_id_type=pl.DeviceIdType.MESH,
+        )
+
+    def send_rows(shift, carry):
+        rows_copy(shift).start()
+        return carry
+
+    lax.fori_loop(1, ring, send_rows, 0)
+    rows_in[0] = normed_ref[...]
+    locals_[0].wait()
+
+    def project(shift, carry):
+        @pl.when(shift > 0)
+        def _():
+            rows_copy(shift).wait_recv()
+
+        share_out[shift] = jnp.dot(
+            rows_in[shift], weight_ref[...], preferred_element_type=full
+        ).astype(half)
+
+        @pl.when(shift > 0)
+        def _():
+            share_copy(shift).start()
+
+        return carry
+
+    lax.fori_loop(0, ring, project, 0)
+    share_in[0] = share_out[0]
+
+    def mix(shift, squares):
+        @pl.when(shift > 0)
+        def _():
+            share_copy(shift).wait_recv()
+
+        column = pl.multiple_of(lax.rem(me + shift, ring) * share, share)
+        values = (
+            residual_ref[:, pl.ds(column, share)].astype(full) + share_in[shift].astype(full)
+        ).astype(half)
+        mixed_ref[:, pl.ds(column, share)] = values
+        wide = values.astype(full)
+        return squares + jnp.sum(wide * wide, axis=1, keepdims=True)
+
+    squares = lax.fori_loop(0, ring, mix, jnp.zeros((mixed_ref.shape[0], 1), full))
+    scale = lax.rsqrt(squares * (1.0 / width) + EPSILON)
+    moe_ref[...] = (mixed_ref[:, :width].astype(full) * scale * gain_ref[...]).astype(half)
+
+    def dispatch(shift, carry):
+        outgoing[shift] = jnp.dot(
+            send_pick_ref[shift], moe_ref[...], preferred_element_type=full
+        ).astype(half)
+
+        @pl.when(shift > 0)
+        def _():
+            out_copy(shift).start()
+
+        return carry
+
+    lax.fori_loop(1, experts, dispatch, 0)
+    arrived[0] = jnp.dot(send_pick_ref[0], moe_ref[...], preferred_element_type=full).astype(half)
+    for copy in locals_[1:]:
+        copy.wait()
+
+    def run_expert(pair, carry):
+        low = pair * 2
+
+        @pl.when(low > 0)
+        def _():
+            out_copy(low).wait_recv()
+
+        out_copy(low + 1).wait_recv()
+        rows = arrived[pl.ds(low, 2)].reshape(2 * capacity, width)
+        gate_part = jnp.dot(rows, gate_ref[...], preferred_element_type=full)
+        up_part = jnp.dot(rows, up_ref[...], preferred_element_type=full)
+        hidden = (gate_part * jax.nn.sigmoid(gate_part) * up_part).astype(half)
+        made = jnp.dot(hidden, down_ref[...], preferred_element_type=full).astype(half)
+        result[pl.ds(low, 2)] = made.reshape(2, capacity, width)
+
+        @pl.when(low > 0)
+        def _():
+            back_copy(low).start()
+
+        back_copy(low + 1).start()
+        return carry
+
+    lax.fori_loop(0, experts // 2, run_expert, 0)
+    returned[0] = result[0]
+
+    def take_back(shift, carry):
+        back_copy(shift).wait_recv()
+        return carry
+
+    lax.fori_loop(1, experts, take_back, 0)
+    first_weight = pair_ref[:, 0:1]
+    second_weight = pair_ref[:, 1:2]
+
+    def combine(tile, carry):
+        column = pl.multiple_of(tile * stretch, stretch)
+        rows = returned[:, :, pl.ds(column, stretch)].reshape(experts * capacity, stretch)
+        first = jnp.dot(first_pick_ref[...], rows, preferred_element_type=full)
+        second = jnp.dot(second_pick_ref[...], rows, preferred_element_type=full)
+        out_ref[:, pl.ds(column, stretch)] = (
+            mixed_ref[:, pl.ds(column, stretch)].astype(full)
+            + first_weight * first
+            + second_weight * second
+        ).astype(half)
+        return carry
+
+    lax.fori_loop(0, width // stretch, combine, 0)
+
+    def drain_seq(shift, carry):
+        rows_copy(shift).wait_send()
+        share_copy(shift).wait_send()
+        return carry
+
+    def drain_grp(shift, carry):
+        out_copy(shift).wait_send()
+        back_copy(shift).wait_send()
+        return carry
+
+    lax.fori_loop(1, ring, drain_seq, 0)
+    lax.fori_loop(1, experts, drain_grp, 0)
 
 
 def on_device(
@@ -32,10 +270,13 @@
     half = jnp.bfloat16
     ring = lax.axis_size("seq")
     own = lax.axis_index("seq")
-    share = out_weight.shape[1] // ring
-    weight_share = lax.all_gather(
-        lax.dynamic_slice_in_dim(out_weight, own * share, share, axis=1), "grp", axis=0, tiled=True
-    )
+    share = -(-out_weight.shape[1] // (ring * 128)) * 128
+    extra = ring * share - out_weight.shape[1]
+    weight_part = lax.dynamic_slice_in_dim(
+        jnp.pad(out_weight, ((0, 0), (0, extra))), own * share, share, axis=1
+    )
+    weight_part, conv_input = lax.optimization_barrier((weight_part, conv_input))
+    weight_share = lax.all_gather(weight_part, "grp", axis=0, tiled=True)
     frames_in = conv_input[0]
     row_count = frames_in.shape[0]
     tap_count = conv_weight.shape[0]
@@ -96,55 +337,70 @@
     normed = (gated_out * lax.rsqrt(mean_square + EPSILON) * norm_gain[None, :]).astype(
         jnp.bfloat16
     )
-    all_rows = lax.all_gather(normed, "seq", axis=0, tiled=True)
-    column_share = jnp.dot(all_rows, weight_share, preferred_element_type=jnp.float32).astype(half)
-    projected = lax.all_to_all(column_share, "seq", split_axis=0, concat_axis=1, tiled=True).astype(
-        jnp.float32
-    )
-    mixed_out = (residual[0].astype(jnp.float32) + projected).astype(jnp.bfloat16)
-    mixed_float = mixed_out.astype(jnp.float32)
-    mixed_square = jnp.mean(mixed_float * mixed_float, axis=1, keepdims=True)
-    moe_in = (mixed_float * lax.rsqrt(mixed_square + EPSILON) * moe_gain[None, :]).astype(
-        jnp.bfloat16
-    )
     experts = lax.axis_size("grp")
     capacity = 4 * row_count // experts
-    flat_picks = routes[0].reshape(-1)
+    flat_picks = (routes[0].reshape(-1) - lax.axis_index("grp") + experts) % experts
     member = (flat_picks[:, None] == jnp.arange(experts)[None, :]).astype(jnp.int32)
     position = jnp.cumsum(member, axis=0) - member
     slot_index = jnp.sum(position * member, axis=1)
     target = (flat_picks * capacity + slot_index).reshape(row_count, 2)
-    selector = jnp.any(
-        target[None, :, :] == jnp.arange(experts * capacity)[:, None, None], axis=2
-    ).astype(jnp.bfloat16)
-    outgoing = (
-        jnp.dot(selector, moe_in, preferred_element_type=jnp.float32)
-        .astype(jnp.bfloat16)
-        .reshape(experts, capacity, model_width)
-    )
-    gate_matrix = w_gate[0]
-    up_matrix = w_up[0]
-    down_matrix = w_down[0]
-    arrived = lax.all_to_all(outgoing, "grp", split_axis=0, concat_axis=0, tiled=True)
-    flattened_rows = arrived.reshape(-1, model_width)
-    gate_part = jnp.dot(flattened_rows, gate_matrix, preferred_element_type=jnp.float32)
-    up_part = jnp.dot(flattened_rows, up_matrix, preferred_element_type=jnp.float32)
-    expert_hidden = (jax.nn.silu(gate_part) * up_part).astype(jnp.bfloat16)
-    result = (
-        jnp.dot(expert_hidden, down_matrix, preferred_element_type=jnp.float32)
-        .astype(jnp.bfloat16)
-        .reshape(arrived.shape)
-    )
-    returned = lax.all_to_all(result, "grp", split_axis=0, concat_axis=0, tiled=True)
-    back_rows = returned.reshape(experts * capacity, model_width)
-    slots = jnp.arange(experts * capacity)[None, :]
-    first_pick = (target[:, 0:1] == slots).astype(half)
-    second_pick = (target[:, 1:2] == slots).astype(half)
-    first_out = jnp.dot(first_pick, back_rows, preferred_element_type=jnp.float32)
-    second = jnp.dot(second_pick, back_rows, preferred_element_type=jnp.float32)
-    pair_weights = route_weights[0]
-    layer_out = mixed_float + pair_weights[:, 0:1] * first_out + pair_weights[:, 1:2] * second
-    return layer_out.astype(jnp.bfloat16)[None]
+    slots = jnp.arange(experts * capacity)
+    send_pick = (
+        jnp.any(target[None, :, :] == slots[:, None, None], axis=2)
+        .astype(half)
+        .reshape(experts, capacity, row_count)
+    )
+    first_pick = (target[:, 0:1] == slots[None, :]).astype(half)
+    second_pick = (target[:, 1:2] == slots[None, :]).astype(half)
+    hidden_width = w_gate.shape[2]
+    vmem = pl.BlockSpec(memory_space=pltpu.VMEM)
+    anywhere = pl.BlockSpec(memory_space=pl.ANY)
+    slab = pltpu.VMEM((experts, capacity, model_width), half)
+    piece = pltpu.VMEM((ring, row_count, share), half)
+    whole_rows = pltpu.VMEM((row_count, model_width), half)
+    layer_out = pl.pallas_call(
+        functools.partial(exchange_kernel, ring, experts),
+        out_shape=jax.ShapeDtypeStruct((row_count, model_width), half),
+        in_specs=[vmem, anywhere, vmem, vmem, anywhere, anywhere, anywhere, vmem, vmem, vmem, vmem],
+        out_specs=vmem,
+        scratch_shapes=[
+            pltpu.VMEM((inner_width, share), half),
+            pltpu.VMEM((model_width, hidden_width), half),
+            pltpu.VMEM((model_width, hidden_width), half),
+            pltpu.VMEM((hidden_width, model_width), half),
+            pltpu.VMEM((ring, row_count, inner_width), half),
+            piece,
+            piece,
+            pltpu.VMEM((row_count, ring * share), half),
+            whole_rows,
+            slab,
+            slab,
+            slab,
+            slab,
+            pltpu.SemaphoreType.DMA((4,)),
+        ]
+        + [pltpu.SemaphoreType.DMA((ring,))] * 4
+        + [pltpu.SemaphoreType.DMA((experts,))] * 4,
+        compiler_params=pltpu.CompilerParams(
+            collective_id=0, has_side_effects=True, vmem_limit_bytes=48 * 1024 * 1024
+        ),
+        cost_estimate=pl.CostEstimate(
+            flops=6 * 1024 * 1024 * 1024, bytes_accessed=64 * 1024 * 1024, transcendentals=0
+        ),
+    )(
+        normed,
+        weight_share,
+        jnp.pad(residual[0], ((0, 0), (0, extra))),
+        moe_gain[None, :],
+        w_gate[0],
+        w_up[0],
+        w_down[0],
+        send_pick,
+        first_pick,
+        second_pick,
+        route_weights[0],
+    )
+    return layer_out[None]
 
 
 def solution(mesh):

time: 338 us -> 250 us (0.74)
  Pallas kernels: 0 us -> 163 us
  waiting for transfers between devices: 180 us -> 28.2 us
  blocking collectives: 68.3 us -> 5.68 us
  matrix products: 25.6 us -> 2.56 us
  starting transfers between devices: 17.8 us -> 9.82 us
    pallas_call x0 -> x1, Pallas kernels: none -> 163 us  [on_device(): pl.pallas_call(functools.partial(exchange_kernel, ring, experts), out_sha...]
    all_gather x2 -> x1, waiting for transfers between devices: 88.9 us -> 4.53 us  [on_device(): weight_share = lax.all_gather(weight_part, 'grp', axis=0, tiled=True)]
    all_to_all x2 -> x0, waiting for transfers between devices: 67.7 us -> none  [the longest x1 58.2 us: on_device(): lax.all_to_all(result, 'grp', split_axis=0, concat_axis=0, tiled=True)]
    all_to_all x1 -> x0, blocking collectives: 62.7 us -> none  [on_device(): lax.all_to_all(outgoing, 'grp', split_axis=0, concat_axis=0, tiled=True)]
    dot_general x6 -> x0, matrix products: 22 us -> none  [the longest x1 7.24 us: on_device(): jnp.dot(expert_hidden, down_matrix, preferred_element_type=jnp.float32)]
    all_to_all x2 -> x0, starting transfers between devices: 8.01 us -> none  [the longest x1 4.52 us: on_device(): lax.all_to_all(result, 'grp', split_axis=0, concat_axis=0, tiled=True)]
  transfers between devices with their start and end apart: 8 -> 5, of which waited for: 6 -> 3; matrix products, arithmetic and copies ran while one was open for 5% -> 9% of each run, Pallas kernels for 0% -> 0%
where the time goes in v2:
time: 250 us
  Pallas kernels  163 us (65%)
  waiting for transfers between devices  28.2 us (11%)
  local copies, waits for them, and re-layouts  17.5 us (7%)
  between operations  13.7 us (5%)
  starting transfers between devices  9.82 us (4%)
  other arithmetic  9.27 us (4%)
  blocking collectives  5.68 us (2%)
  matrix products  2.56 us (1%)
    pallas_call x1, Pallas kernels, on_device(): pl.pallas_call(functools.partial(exchange_kernel, ring, experts), out_sha...  163 us
    ppermute x4, waiting for transfers between devices, from_behind(): lax.ppermute(value, axis, [(source, source + steps) for source in range(f...  23.6 us
    ppermute x4, starting transfers between devices, from_behind(): lax.ppermute(value, axis, [(source, source + steps) for source in range(f...  9.78 us
    all_gather x1, blocking collectives, on_device(): totals = lax.all_gather(cumulative[-1], 'seq', axis=0)  5.68 us
  transfers between devices with their start and end apart: 5, of which 3 were waited for; matrix products, arithmetic and copies ran while one was open for 9% of the time, Pallas kernels for 0%

profile of v2, /device:TPU:0, one launch (start us, length us, event | category | flops | bytes accessed | tf_op | source)
XLA Modules:
  0.0 249.9 jit_solution(8167818080294532223)
XLA Ops:
  6.5 0.0 all-gather.3.cloned.1.call-start
  6.6 1.4 copy-done
  8.0 0.8 constant_dynamic-slice_fusion.2
  8.8 1.4 slice_bitcast_fusion
  10.2 3.0 %collective-permute-start = (bf16[3,2688]{1,0:T(4,128)(2,1)}, bf16[3,2688]{1,0:T(4,128)(2,1)}, u32[]{:S(2)}, u32[]{:S(2)}) collective-permute-start(bf16[3,2688]{1,0:T(4,128)(2,1)} %slice_bitcast_fusion), channel_id=1, source_target_pairs={{0,8},{8,16},{16,24},{1,9},{9,17},{17,25},{2,10},{10,18},{18,26},{... | collective-permute-start | bytes 48392 | tf_op jit(solution)/shard_map/ppermute | solution.py:16
  13.1 0.0 all-gather.3.cloned.1.call-update
  13.2 0.7 subtract_add_fusion
  13.9 0.1 copy.92
  14.0 0.1 add.141
  14.1 0.1 add.138
  14.3 0.6 reduce-window.6
  14.9 0.2 slice_reduce_fusion.4
  15.1 0.1 fusion.38
  15.2 0.1 reduce_sum.25
  15.4 0.1 reduce_sum.24
  15.5 0.1 copy.84
  15.7 0.1 copy.95
  15.7 0.1 copy.94
  15.8 0.1 negate_multiply_fusion
  15.9 0.0 copy-start.3
  15.9 0.2 reduce_window_sum.26
  16.1 5.7 %all-gather = f32[4,1,40]{2,1,0:T(1,128)S(1)} all-gather(f32[1,1,40]{2,1,0:T(1,128)S(1)} %get-tuple-element.13), channel_id=1, replica_groups=mesh['seq'=4,'grp'=8] {'seq'}, dimensions={0}, use_global_device_ids=true | all-gather | bytes 800 | tf_op jit(solution)/shard_map/all_gather | solution.py:320
  21.7 0.6 iota_compare_fusion.3
  22.4 0.0 copy-done.16
  22.4 0.1 fusion.23
  22.4 0.7 slice_reduce_fusion.3
  23.2 0.1 fusion.24
  23.3 0.7 fusion.54
  24.0 0.6 exponential_bitcast_fusion
  24.6 1.4 copy.82
  26.1 1.5 copy.87
  27.6 0.7 copy.85
  28.3 0.1 copy.88
  28.3 0.7 copy.89
  29.0 1.3 copy.91
  30.4 0.1 copy.96
  30.5 0.7 broadcast_in_dim.24.gain_ref
  31.2 0.0 collective-permute-done
  31.2 1.2 copy.83
  32.4 0.6 maximum_convert_fusion
  33.0 0.1 copy-done.6
  33.1 0.0 copy-done.7
  33.1 0.0 copy-done.8
  33.1 2.9 %multiply_convert_fusion.1 = bf16[128,2688]{0,1:T(8,128)(2,1)S(1)} fusion(f32[131,2688]{0,1:T(8,128)S(1)} %maximum_convert_fusion, f32[2688]{0:T(1024)S(1)} %copy-done.7, f32[2688]{0:T(1024)S(1)} %copy-done.8, f32[2688]{0:T(1024)S(1)} %copy-done.6, f32[2688]{0:T(1024)S(1)} %get-tuple-element.9), kind=kLoop, calls=%fused_computation.15 | loop fusion | flops 4128768 | bytes 6236160 | tf_op jit(solution)/shard_map/convert_element_type | solution.py:295
  36.0 0.0 copy-start.12
  36.0 0.0 copy-start.13
  36.0 0.0 copy-start.14
  36.1 0.3 convolution_convert_fusion
  36.4 2.2 collective-permute-start.1
  38.6 3.3 %collective-permute-start.2 = (bf16[40,64,64]{2,1,0:T(8,128)(2,1)S(1)}, bf16[40,64,64]{2,1,0:T(8,128)(2,1)S(1)}, u32[]{:S(2)}, u32[]{:S(2)}) collective-permute-start(bf16[40,64,64]{2,1,0:T(8,128)(2,1)S(1)} %convolution_convert_fusion), channel_id=1, source_target_pairs={{0,16},{8,24},{1,17},{9,25},{2,18},{10,26},{3,19},{11,27},{4,20},{... | collective-permute-start | bytes 983048 | tf_op jit(solution)/shard_map/ppermute | solution.py:16
  41.9 1.3 collective-permute-start.3
  43.3 0.2 fusion.33
  43.5 0.0 copy-start.20
  43.5 1.1 convolution_bitcast_fusion
  44.6 0.0 collective-permute-done.1
  44.6 12.4 %collective-permute-done.2 = bf16[40,64,64]{2,1,0:T(8,128)(2,1)S(1)} collective-permute-done((bf16[40,64,64]{2,1,0:T(8,128)(2,1)S(1)}, bf16[40,64,64]{2,1,0:T(8,128)(2,1)S(1)}, u32[]{:S(2)}, u32[]{:S(2)}) %collective-permute-start.2) | collective-permute-done | bytes 327712 | tf_op jit(solution)/shard_map/ppermute | solution.py:16
  57.1 11.2 %collective-permute-done.3 = bf16[40,64,64]{2,1,0:T(8,128)(2,1)S(1)} collective-permute-done((bf16[40,64,64]{2,1,0:T(8,128)(2,1)S(1)}, bf16[40,64,64]{2,1,0:T(8,128)(2,1)S(1)}, u32[]{:S(2)}, u32[]{:S(2)}) %collective-permute-start.3) | collective-permute-done | bytes 327712 | tf_op jit(solution)/shard_map/ppermute | solution.py:16
  68.3 1.0 multiply_reduce_fusion
  69.2 1.5 copy.90
  70.7 2.0 fusion.17.normed_ref
  72.7 4.5 %all-gather.3.cloned.1.call-done.weight_hbm = bf16[2560,640]{1,0:T(8,128)(2,1)} async-done(((bf16[320,640]{1,0:T(8,128)(2,1)}), bf16[2560,640]{1,0:T(8,128)(2,1)}) %all-gather.3.cloned.1.call-update) | async-done | bytes 3276816 | tf_op jit(solution)/shard_map/all_gather | solution.py:279
  77.3 1.7 copy-done.1
  79.0 163.2 %shard_map.145 = bf16[128,2560]{1,0:T(8,128)(2,1)S(1)} custom-call(bf16[128,2560]{1,0:T(8,128)(2,1)S(1)} %fusion.17.normed_ref, bf16[2560,640]{1,0:T(8,128)(2,1)} %all-gather.3.cloned.1.call-done.weight_hbm, bf16[128,2560]{1,0:T(8,128)(2,1)S(1)} %bitcast.96, f32[1,2560]{1,0:T(1,128)S(1)} %broadcast_in_dim.24.gain_ref, bf16[2560,512]{1,0:T(8,128)(2,1)S(1)} %bitcast.95, ...), custom_call_target="tpu_custom_call" | custom-call | flops 6442450944 | bytes 67108864 | tf_op jit(solution)/shard_map/pallas_call | solution.py:361
  242.2 0.8 copy.98
  (44 shorter events, 0.2 us)
Async XLA Ops:
  6.5 1.5 copy-start
  6.5 15.8 %copy-start.16 = (s32[1,128,2]{1,2,0:T(2,128)S(1)}, s32[1,128,2]{1,2,0:T(2,128)}, u32[]{:S(2)}) copy-start(s32[1,128,2]{1,2,0:T(2,128)} %param.28) | copy-start | bytes 3076
  6.5 9.0 %copy-start.10 = (f32[1,128,40]{1,2,0:T(8,128)S(1)}, f32[1,128,40]{1,2,0:T(8,128)}, u32[]{:S(2)}) copy-start(f32[1,128,40]{1,2,0:T(8,128)} %param.17) | copy-start | bytes 61444
  6.5 9.1 %copy-start.19 = (f32[40]{0:T(128)S(1)}, f32[40]{0:T(128)}, u32[]{:S(2)}) copy-start(f32[40]{0:T(128)} %param.18) | copy-start | bytes 484
  6.5 15.9 %copy-start.9 = (f32[4,2688]{1,0:T(4,128)S(1)}, f32[4,2688]{1,0:T(4,128)}, u32[]{:S(2)}) copy-start(f32[4,2688]{1,0:T(4,128)} %param.16) | copy-start | bytes 129028
  6.5 70.7 %all-gather.3.cloned.1.call-start = ((), (), s32[]{:S(2)}) async-start(), calls=%async_computation | async-start | bytes 3686400 | tf_op jit(solution)/shard_map/all_gather | solution.py:279
  10.2 21.0 %collective-permute-start = (bf16[3,2688]{1,0:T(4,128)(2,1)}, bf16[3,2688]{1,0:T(4,128)(2,1)}, u32[]{:S(2)}, u32[]{:S(2)}) collective-permute-start(bf16[3,2688]{1,0:T(4,128)(2,1)} %slice_bitcast_fusion), channel_id=1, source_target_pairs={{0,8},{8,16},{16,24},{1,9},{9,17},{17,25},{2,10},{10,18},{18,26},{... | collective-permute-start | bytes 48392 | tf_op jit(solution)/shard_map/ppermute | solution.py:16
  15.9 13.2 %copy-start.3 = (bf16[1,128,2560]{2,1,0:T(8,128)(2,1)S(1)}, bf16[1,128,2560]{2,1,0:T(8,128)(2,1)}, u32[]{:S(2)}) copy-start(bf16[1,128,2560]{2,1,0:T(8,128)(2,1)} %param.20) | copy-start | bytes 1966084
  24.0 4.3 %copy-start.5 = (f32[128,40]{1,0:T(8,128)S(1)}, f32[128,40]{1,0:T(8,128)}, u32[]{:S(2)}) copy-start(f32[128,40]{1,0:T(8,128)} %get-tuple-element.16) | copy-start | bytes 61444
  26.0 4.3 %copy-start.17 = (f32[1,128,2]{1,2,0:T(2,128)S(1)}, f32[1,128,2]{1,2,0:T(2,128)}, u32[]{:S(2)}) copy-start(f32[1,128,2]{1,2,0:T(2,128)} %param.29) | copy-start | bytes 3076
  32.4 0.7 copy-start.6
  32.4 0.7 copy-start.7
  32.4 0.7 copy-start.8
  36.0 7.4 %copy-start.12 = (f32[40,128]{1,0:T(8,128)S(1)}, f32[40,128]{1,0:T(8,128)}, u32[]{:S(2)}) copy-start(f32[40,128]{1,0:T(8,128)} %copy.87) | copy-start | bytes 61444
  36.0 7.4 %copy-start.13 = (f32[40,128]{1,0:T(8,128)S(1)}, f32[40,128]{1,0:T(8,128)}, u32[]{:S(2)}) copy-start(f32[40,128]{1,0:T(8,128)} %copy.85) | copy-start | bytes 61444
  36.0 7.4 %copy-start.14 = (pred[128,128]{1,0:T(8,128)(4,1)S(1)}, pred[128,128]{1,0:T(8,128)(4,1)}, u32[]{:S(2)}) copy-start(pred[128,128]{1,0:T(8,128)(4,1)} %iota_compare_fusion.3) | copy-start | bytes 49156
  36.4 8.2 %collective-permute-start.1 = (bf16[40,64,64]{2,1,0:T(8,128)(2,1)S(1)}, bf16[40,64,64]{2,1,0:T(8,128)(2,1)S(1)}, u32[]{:S(2)}, u32[]{:S(2)}) collective-permute-start(bf16[40,64,64]{2,1,0:T(8,128)(2,1)S(1)} %convolution_convert_fusion), channel_id=1, source_target_pairs={{0,8},{8,16},{16,24},{1,9},{9,17},{17,25},{2,10},{10,18},{18,26},{... | collective-permute-start | bytes 983048 | tf_op jit(solution)/shard_map/ppermute | solution.py:16
  38.6 18.5 %collective-permute-start.2 = (bf16[40,64,64]{2,1,0:T(8,128)(2,1)S(1)}, bf16[40,64,64]{2,1,0:T(8,128)(2,1)S(1)}, u32[]{:S(2)}, u32[]{:S(2)}) collective-permute-start(bf16[40,64,64]{2,1,0:T(8,128)(2,1)S(1)} %convolution_convert_fusion), channel_id=1, source_target_pairs={{0,16},{8,24},{1,17},{9,25},{2,18},{10,26},{3,19},{11,27},{4,20},{... | collective-permute-start | bytes 983048 | tf_op jit(solution)/shard_map/ppermute | solution.py:16
  41.9 26.3 %collective-permute-start.3 = (bf16[40,64,64]{2,1,0:T(8,128)(2,1)S(1)}, bf16[40,64,64]{2,1,0:T(8,128)(2,1)S(1)}, u32[]{:S(2)}, u32[]{:S(2)}) collective-permute-start(bf16[40,64,64]{2,1,0:T(8,128)(2,1)S(1)} %convolution_convert_fusion), channel_id=1, source_target_pairs={{0,24},{1,25},{2,26},{3,27},{4,28},{5,29},{6,30},{7,31}} | collective-permute-start | bytes 983048 | tf_op jit(solution)/shard_map/ppermute | solution.py:16
  43.5 24.8 %copy-start.4 = (f32[1,128,2560]{1,2,0:T(8,128)S(1)}, f32[1,128,2560]{1,2,0:T(8,128)}, u32[]{:S(2)}) copy-start(f32[1,128,2560]{1,2,0:T(8,128)} %copy.91) | copy-start | bytes 3932164
  43.5 24.8 %copy-start.11 = (f32[128,40]{0,1:T(8,128)S(1)}, f32[128,40]{0,1:T(8,128)}, u32[]{:S(2)}) copy-start(f32[128,40]{0,1:T(8,128)} %copy.89) | copy-start | bytes 61444
  43.5 24.8 %copy-start.18 = (f32[40]{0:T(128)S(1)}, f32[40]{0:T(128)}, u32[]{:S(2)}) copy-start(f32[40]{0:T(128)} %get-tuple-element.19) | copy-start | bytes 484
  43.5 24.7 %copy-start.20 = (f32[40]{0:T(128)S(1)}, f32[40]{0:T(128)}, u32[]{:S(2)}) copy-start(f32[40]{0:T(128)} %param.19) | copy-start | bytes 484
  69.2 1.5 copy-start.15
  70.7 6.6 %copy-start.2 = (bf16[1,128,2560]{2,1,0:T(8,128)(2,1)S(1)}, bf16[1,128,2560]{2,1,0:T(8,128)(2,1)}, u32[]{:S(2)}) copy-start(bf16[1,128,2560]{2,1,0:T(8,128)(2,1)} %param.23) | copy-start | bytes 1966084
  77.3 1.7 copy-start.1
Sparse Core Ops, SparseCore 0:
  13.3 63.9 all-gather.2

commit v3 on v2

--- a/solution.py
+++ b/solution.py
@@ -16,10 +16,106 @@
     return lax.ppermute(value, axis, [(source, source + steps) for source in range(first, last)])
 
 
+def mixer_kernel(
+    chips,
+    state_ref,
+    reach_ref,
+    c_ref,
+    base_ref,
+    fade_ref,
+    gate_ref,
+    gain_ref,
+    rows_ref,
+    gated,
+    states,
+    near_state_send,
+    far_state_send,
+    state_recv,
+    near_rows_send,
+    far_rows_send,
+    rows_recv,
+):
+    me = lax.axis_index("seq")
+    chip, core = me // 2, me % 2
+    twin = chip * 2 + 1 - core
+    half = jnp.bfloat16
+    full = jnp.float32
+
+    def far(step):
+        return lax.rem(chip + step, chips) * 2 + core
+
+    barrier = pltpu.get_barrier_semaphore()
+
+    def greet(device):
+        pl.semaphore_signal(
+            barrier, inc=1, device_id={"seq": device}, device_id_type=pl.DeviceIdType.MESH
+        )
+
+    greet(twin)
+    for step in range(1, chips):
+        greet(far(step))
+    pl.semaphore_wait(barrier, chips)
+
+    def copy(slots, near_send, far_send, recv, step, near):
+        return pltpu.make_async_remote_copy(
+            src_ref=slots.at[2 * step] if near else slots.at[0],
+            dst_ref=slots.at[2 * step + 1] if near else slots.at[2 * step],
+            send_sem=near_send.at[step] if near else far_send.at[step],
+            recv_sem=recv.at[2 * step + 1] if near else recv.at[2 * step],
+            device_id={"seq": twin if near else far(step)},
+            device_id_type=pl.DeviceIdType.MESH,
+        )
+
+    def exchange(*parts):
+        for step in range(1, chips):
+            copy(*parts, step, False).start()
+        copy(*parts, 0, True).start()
+        for step in range(1, chips):
+            copy(*parts, step, False).wait_recv()
+            copy(*parts, step, True).start()
+        for step in range(chips):
+            copy(*parts, step, True).wait_recv()
+
+    def drain(*parts):
+        for step in range(1, chips):
+            copy(*parts, step, False).wait_send()
+        for step in range(chips):
+            copy(*parts, step, True).wait_send()
+
+    state_parts = (states, near_state_send, far_state_send, state_recv)
+    rows_parts = (rows_ref, near_rows_send, far_rows_send, rows_recv)
+    states[0] = state_ref[...]
+    exchange(*state_parts)
+    width = gate_ref.shape[1]
+    stretch = 512 if width % 512 == 0 else 128
+    squares = jnp.zeros((gate_ref.shape[0], 1), full)
+    for start in range(0, width, stretch):
+        columns = slice(start, start + stretch)
+        entering = jnp.zeros((states.shape[1], stretch), full)
+        for slot in range(1, 2 * chips):
+            entering = entering + reach_ref[slot : slot + 1, columns] * states[
+                slot, :, columns
+            ].astype(full)
+        carried = jnp.dot(c_ref[...], entering.astype(half), preferred_element_type=full)
+        gate = gate_ref[:, columns].astype(full)
+        value = (base_ref[:, columns] + carried * fade_ref[:, columns]) * (
+            gate * jax.nn.sigmoid(gate)
+        )
+        gated[:, columns] = value
+        squares = squares + jnp.sum(value * value, axis=1, keepdims=True)
+    scale = lax.rsqrt(squares * (1.0 / width) + EPSILON)
+    for start in range(0, width, stretch):
+        columns = slice(start, start + stretch)
+        rows_ref[0, :, columns] = (gated[:, columns] * scale * gain_ref[:, columns]).astype(half)
+    exchange(*rows_parts)
+    drain(*state_parts)
+    drain(*rows_parts)
+
+
 def exchange_kernel(
     ring,
     experts,
-    normed_ref,
+    rows_ref,
     weight_hbm,
     residual_ref,
     gain_ref,
@@ -35,7 +131,6 @@
     gate_ref,
     up_ref,
     down_ref,
-    rows_in,
     share_out,
     share_in,
     mixed_ref,
@@ -45,8 +140,6 @@
     result,
     returned,
     local_sem,
-    rows_send,
-    rows_recv,
     share_send,
     share_recv,
     out_send,
@@ -90,23 +183,28 @@
     greet("grp", mine, experts)
     pl.semaphore_wait(barrier, ring - 1 + experts - 1)
 
-    def rows_copy(shift):
+    def source(slot):
+        chips = ring // 2
+        chip = lax.rem(me // 2 + chips - slot // 2, chips)
+        return chip * 2 + lax.rem(me + slot, 2)
+
+    def share_copy(slot):
         return pltpu.make_async_remote_copy(
-            src_ref=normed_ref,
-            dst_ref=rows_in.at[shift],
-            send_sem=rows_send.at[shift],
-            recv_sem=rows_recv.at[shift],
-            device_id={"seq": lax.rem(me + shift, ring)},
+            src_ref=share_out.at[slot],
+            dst_ref=share_in.at[me],
+            send_sem=share_send.at[slot],
+            recv_sem=share_recv.at[me],
+            device_id={"seq": source(slot)},
             device_id_type=pl.DeviceIdType.MESH,
         )
 
-    def share_copy(shift):
+    def share_arrival(column):
         return pltpu.make_async_remote_copy(
-            src_ref=share_out.at[shift],
-            dst_ref=share_in.at[shift],
-            send_sem=share_send.at[shift],
-            recv_sem=share_recv.at[shift],
-            device_id={"seq": lax.rem(me + ring - shift, ring)},
+            src_ref=share_out.at[0],
+            dst_ref=share_in.at[column],
+            send_sem=share_send.at[0],
+            recv_sem=share_recv.at[column],
+            device_id={"seq": source(1)},
             device_id_type=pl.DeviceIdType.MESH,
         )
 
@@ -130,40 +228,31 @@
             device_id_type=pl.DeviceIdType.MESH,
         )
 
-    def send_rows(shift, carry):
-        rows_copy(shift).start()
-        return carry
-
-    lax.fori_loop(1, ring, send_rows, 0)
-    rows_in[0] = normed_ref[...]
     locals_[0].wait()
 
-    def project(shift, carry):
-        @pl.when(shift > 0)
+    def project(index, carry):
+        slot = ring - 1 - index
+        share_out[slot] = jnp.dot(
+            rows_ref[slot], weight_ref[...], preferred_element_type=full
+        ).astype(half)
+
+        @pl.when(slot > 0)
         def _():
-            rows_copy(shift).wait_recv()
-
-        share_out[shift] = jnp.dot(
-            rows_in[shift], weight_ref[...], preferred_element_type=full
-        ).astype(half)
-
-        @pl.when(shift > 0)
+            share_copy(slot).start()
+
+        return carry
+
+    lax.fori_loop(0, ring, project, 0)
+    share_in[me] = share_out[0]
+
+    def mix(index, squares):
+        @pl.when(index != me)
         def _():
-            share_copy(shift).start()
-
-        return carry
-
-    lax.fori_loop(0, ring, project, 0)
-    share_in[0] = share_out[0]
-
-    def mix(shift, squares):
-        @pl.when(shift > 0)
-        def _():
-            share_copy(shift).wait_recv()
-
-        column = pl.multiple_of(lax.rem(me + shift, ring) * share, share)
+            share_arrival(index).wait_recv()
+
+        column = pl.multiple_of(index * share, share)
         values = (
-            residual_ref[:, pl.ds(column, share)].astype(full) + share_in[shift].astype(full)
+            residual_ref[:, pl.ds(column, share)].astype(full) + share_in[index].astype(full)
         ).astype(half)
         mixed_ref[:, pl.ds(column, share)] = values
         wide = values.astype(full)
@@ -237,7 +326,6 @@
     lax.fori_loop(0, width // stretch, combine, 0)
 
     def drain_seq(shift, carry):
-        rows_copy(shift).wait_send()
         share_copy(shift).wait_send()
         return carry
 
@@ -299,9 +387,7 @@
     step_size = jax.nn.softplus(step_raw[0])
     log_decay = -step_size * jnp.exp(rate_log)[None, :]
     cumulative = jnp.cumsum(log_decay, axis=0)
-    x_values = x_part.astype(jnp.float32).reshape(row_count, head_count, head_width)
-    b_values = b_part.astype(jnp.float32)
-    c_values = c_part.astype(jnp.float32)
+    x_float = x_part.astype(jnp.float32)
     scores = jnp.dot(c_part, b_part.T, preferred_element_type=jnp.float32)
     positions = jnp.arange(row_count)
     causal = positions[:, None] >= positions[None, :]
@@ -311,31 +397,50 @@
     mixing = (scores[None] * decay_mask * step_size.T[:, None, :]).astype(half)
     x_heads = x_part.reshape(row_count, head_count, head_width)
     tail_weight = jnp.exp(cumulative[-1][None, :] - cumulative) * step_size
-    local_state = jnp.einsum(
-        "shp,sn->hpn",
-        (x_values * tail_weight[:, :, None]).astype(half),
+    local_state = lax.dot_general(
         b_part,
+        (x_float * jnp.repeat(tail_weight, head_width, axis=1)).astype(half),
+        (((0,), (0,)), ((), ())),
         preferred_element_type=jnp.float32,
     ).astype(half)
     totals = lax.all_gather(cumulative[-1], "seq", axis=0)
-    passing = jnp.zeros_like(totals[0])
-    entering = jnp.zeros(local_state.shape, jnp.float32)
-    for shift in range(1, ring):
-        arrived_state = from_behind(local_state, "seq", shift).astype(jnp.float32)
-        entering = entering + jnp.exp(passing)[:, None, None] * arrived_state
-        passing = passing + totals[jnp.maximum(own - shift, 0)]
+    slot_ids = jnp.arange(ring)
+    origin = (own // 2 - slot_ids // 2 + ring // 2) % (ring // 2) * 2 + (own + slot_ids) % 2
+    between = (slot_ids[None, :] > origin[:, None]) & (slot_ids[None, :] < own)
+    passed = jnp.sum(jnp.where(between[:, :, None], totals[None], 0.0), axis=1)
+    reach = jnp.where((origin < own)[:, None], jnp.exp(passed), 0.0)
     within = jnp.einsum("hts,shp->thp", mixing, x_heads, preferred_element_type=jnp.float32)
-    carried = (
-        jnp.einsum("tn,hpn->thp", c_part, entering.astype(half), preferred_element_type=jnp.float32)
-        * jnp.exp(cumulative)[:, :, None]
-    )
-    ssd_out = (within + carried + skip_gain[None, :, None] * x_values).reshape(
-        row_count, inner_width
-    )
-    gated_out = ssd_out * jax.nn.silu(gate_input[0].astype(jnp.float32))
-    mean_square = jnp.mean(gated_out * gated_out, axis=1, keepdims=True)
-    normed = (gated_out * lax.rsqrt(mean_square + EPSILON) * norm_gain[None, :]).astype(
-        jnp.bfloat16
+    base = within.reshape(row_count, inner_width) + jnp.repeat(skip_gain, head_width)[None, :] * x_float
+    vmem = pl.BlockSpec(memory_space=pltpu.VMEM)
+    all_rows = pl.pallas_call(
+        functools.partial(mixer_kernel, ring // 2),
+        out_shape=jax.ShapeDtypeStruct((ring, row_count, inner_width), half),
+        in_specs=[vmem] * 7,
+        out_specs=vmem,
+        scratch_shapes=[
+            pltpu.VMEM((row_count, inner_width), jnp.float32),
+            pltpu.VMEM((ring, state_width, inner_width), half),
+        ]
+        + [
+            pltpu.SemaphoreType.DMA((ring // 2,)),
+            pltpu.SemaphoreType.DMA((ring // 2,)),
+            pltpu.SemaphoreType.DMA((ring,)),
+        ]
+        * 2,
+        compiler_params=pltpu.CompilerParams(
+            collective_id=1, has_side_effects=True, vmem_limit_bytes=32 * 1024 * 1024
+        ),
+        cost_estimate=pl.CostEstimate(
+            flops=1024 * 1024 * 1024, bytes_accessed=64 * 1024 * 1024, transcendentals=0
+        ),
+    )(
+        local_state,
+        jnp.repeat(reach, head_width, axis=1),
+        c_part,
+        base,
+        jnp.repeat(jnp.exp(cumulative), head_width, axis=1),
+        gate_input[0],
+        norm_gain[None, :],
     )
     experts = lax.axis_size("grp")
     capacity = 4 * row_count // experts
@@ -353,7 +458,6 @@
     first_pick = (target[:, 0:1] == slots[None, :]).astype(half)
     second_pick = (target[:, 1:2] == slots[None, :]).astype(half)
     hidden_width = w_gate.shape[2]
-    vmem = pl.BlockSpec(memory_space=pltpu.VMEM)
     anywhere = pl.BlockSpec(memory_space=pl.ANY)
     slab = pltpu.VMEM((experts, capacity, model_width), half)
     piece = pltpu.VMEM((ring, row_count, share), half)
@@ -368,7 +472,6 @@
             pltpu.VMEM((model_width, hidden_width), half),
             pltpu.VMEM((model_width, hidden_width), half),
             pltpu.VMEM((hidden_width, model_width), half),
-            pltpu.VMEM((ring, row_count, inner_width), half),
             piece,
             piece,
             pltpu.VMEM((row_count, ring * share), half),
@@ -379,7 +482,7 @@
             slab,
             pltpu.SemaphoreType.DMA((4,)),
         ]
-        + [pltpu.SemaphoreType.DMA((ring,))] * 4
+        + [pltpu.SemaphoreType.DMA((ring,))] * 2
         + [pltpu.SemaphoreType.DMA((experts,))] * 4,
         compiler_params=pltpu.CompilerParams(
             collective_id=0, has_side_effects=True, vmem_limit_bytes=48 * 1024 * 1024
@@ -388,7 +491,7 @@
             flops=6 * 1024 * 1024 * 1024, bytes_accessed=64 * 1024 * 1024, transcendentals=0
         ),
     )(
-        normed,
+        all_rows,
         weight_share,
         jnp.pad(residual[0], ((0, 0), (0, extra))),
         moe_gain[None, :],

time: 250 us -> 229 us (0.916)
  waiting for transfers between devices: 28.2 us -> 0.02 us
  local copies, waits for them, and re-layouts: 17.5 us -> 25.1 us
  starting transfers between devices: 9.82 us -> 2.98 us
  Pallas kernels: 163 us -> 168 us
  matrix products: 2.56 us -> 6.57 us
  other arithmetic: 9.27 us -> 5.85 us
    pallas_call x0 -> x1, Pallas kernels: none -> 30.3 us  [on_device(): pl.pallas_call(functools.partial(mixer_kernel, ring // 2), out_shape=jax....]
    pallas_call x1, Pallas kernels: 163 us -> 138 us  [on_device(): pl.pallas_call(functools.partial(exchange_kernel, ring, experts), out_sha...]
    ppermute x4 -> x1, waiting for transfers between devices: 23.6 us -> 0.01 us  [from_behind(): lax.ppermute(value, axis, [(source, source + steps) for source in range(f...]
    ppermute x4 -> x1, starting transfers between devices: 9.78 us -> 2.95 us  [from_behind(): lax.ppermute(value, axis, [(source, source + steps) for source in range(f...]
    reshape x1 -> x4, local copies, waits for them, and re-layouts: 1.47 us -> 6.1 us  [the longest x1 2.8 us: on_device(): within.reshape(row_count, inner_width)]
    all_gather x1, waiting for transfers between devices: 4.53 us -> 0.01 us  [on_device(): weight_share = lax.all_gather(weight_part, 'grp', axis=0, tiled=True)]
    unnamed x46 -> x36, local copies, waits for them, and re-layouts: 4.43 us -> 8.13 us
    slice x1 -> x2, local copies, waits for them, and re-layouts: 0.04 us -> 3.14 us  [on_device(): x_part = signal[:, :inner_width]]
  transfers between devices with their start and end apart: 5 -> 2, of which waited for: 3 -> 0; matrix products, arithmetic and copies ran while one was open for 9% -> 12% of each run, Pallas kernels for 0% -> 13%
where the time goes in v3:
time: 229 us; the launch traced here: 228 us
  Pallas kernels  168 us (73%)
  local copies, waits for them, and re-layouts  25.1 us (11%)
  between operations  13.7 us (6%)
  matrix products  6.57 us (3%)
  other arithmetic  5.85 us (3%)
  blocking collectives  5.7 us (2%)
  starting transfers between devices  2.98 us (1%)
    pallas_call x1, Pallas kernels, on_device(): pl.pallas_call(functools.partial(exchange_kernel, ring, experts), out_sha...  138 us
    pallas_call x1, Pallas kernels, on_device(): pl.pallas_call(functools.partial(mixer_kernel, ring // 2), out_shape=jax....  30.3 us
    unnamed x36, local copies, waits for them, and re-layouts  8.13 us
    all_gather x1, blocking collectives, on_device(): totals = lax.all_gather(cumulative[-1], 'seq', axis=0)  5.7 us
  transfers between devices with their start and end apart: 2, of which 0 were waited for; matrix products, arithmetic and copies ran while one was open for 12% of the time, Pallas kernels for 13%

profile of v3, /device:TPU:0, one launch (start us, length us, event | category | flops | bytes accessed | tf_op | source)
XLA Modules:
  0.0 228.3 jit_solution(4772173217821675467)
XLA Ops:
  6.5 0.0 all-gather.3.cloned.1.call-start
  6.6 1.4 copy-done
  8.0 0.8 constant_dynamic-slice_fusion
  8.8 1.4 slice_bitcast_fusion
  10.2 2.9 %collective-permute-start = (bf16[3,2688]{1,0:T(4,128)(2,1)}, bf16[3,2688]{1,0:T(4,128)(2,1)}, u32[]{:S(2)}, u32[]{:S(2)}) collective-permute-start(bf16[3,2688]{1,0:T(4,128)(2,1)} %slice_bitcast_fusion), channel_id=1, source_target_pairs={{0,8},{8,16},{16,24},{1,9},{9,17},{17,25},{2,10},{10,18},{18,26},{... | collective-permute-start | bytes 48392 | tf_op jit(solution)/shard_map/ppermute | solution.py:16
  13.2 0.0 all-gather.3.cloned.1.call-update
  13.2 0.7 subtract_add_fusion
  13.9 0.1 copy.87
  14.0 0.1 add.162
  14.1 0.1 add.159
  14.3 0.6 reduce-window.6
  14.9 0.2 slice_reduce_fusion.4
  15.1 0.1 fusion.24
  15.2 0.1 reduce_sum.25
  15.4 0.1 reduce_sum.24
  15.5 0.1 copy.77
  15.7 0.1 copy.90
  15.7 0.1 copy.89
  15.8 0.1 negate_multiply_fusion
  15.9 0.2 reduce_window_sum.26
  16.1 5.7 %all-gather = f32[4,1,40]{2,1,0:T(1,128)S(1)} all-gather(f32[1,1,40]{2,1,0:T(1,128)S(1)} %get-tuple-element.16), channel_id=1, replica_groups=mesh['seq'=4,'grp'=8] {'seq'}, dimensions={0}, use_global_device_ids=true | all-gather | bytes 800 | tf_op jit(solution)/shard_map/all_gather | solution.py:406
  21.8 0.1 fusion.27
  21.9 0.1 select_reduce_fusion
  22.0 0.1 fusion.13
  22.1 0.7 slice_reduce_fusion.3
  22.8 0.1 exponential_select_fusion
  22.9 0.1 fusion.14
  23.0 0.1 fusion.46
  23.0 0.6 iota_compare_fusion.3
  23.7 0.7 copy.83
  24.3 0.7 copy.81
  25.0 0.1 broadcast_in_dim.100
  25.1 0.1 mul.135
  25.1 0.1 broadcast_in_dim.97
  25.2 0.1 reshape.172.reach_ref
  25.3 0.1 copy.78
  25.4 0.1 broadcast_in_dim.91
  25.5 1.5 copy.79
  27.0 0.1 copy.85
  27.0 1.2 broadcast_in_dim.101
  28.2 1.7 copy.86.fade_ref
  30.0 0.1 copy.91
  30.2 0.7 broadcast_in_dim.103.gain_ref
  30.9 0.0 collective-permute-done
  30.9 1.3 maximum_convert_fusion
  32.2 1.6 multiply_convert_fusion.1
  33.8 1.0 slice.78
  34.7 0.1 copy-done.5
  34.8 0.1 slice.80.c_ref
  34.9 2.2 copy.80
  37.1 1.0 fusion.20
  38.1 0.0 copy-done.10
  38.1 3.3 %fusion.3 = f32[40,64,128]{2,1,0:T(8,128)} fusion(bf16[128,40,64]{0,2,1:T(8,128)(2,1)} %bitcast.73, f32[40,128]{1,0:T(8,128)S(1)} %copy-done.10, f32[40,128]{1,0:T(8,128)} %copy.81, f32[128,128]{1,0:T(8,128)S(1)} %fusion.20, pred[128,128]{1,0:T(8,128)(4,1)} %iota_compare_fusion.3), kind=kOutput, calls=%fused_computation.12 | convolution fusion | flops 87818240 | bytes 2088960 | tf_op jit(solution)/shard_map/hts,shp->thp/dot_general | solution.py:412
  41.4 2.8 %copy.84 = f32[128,2560]{1,0:T(8,128)} copy(f32[128,2560]{0,1:T(8,128)} %bitcast.71) | data formatting | bytes 2621440 | tf_op jit(solution)/shard_map/reshape | solution.py:413
  44.2 2.3 convolution_convert_fusion.state_ref
  46.5 0.3 copy-done.7
  46.8 0.2 fusion.5.base_ref
  46.9 0.9 copy-done.3
  47.9 30.3 %shard_map.145.rows_ref = bf16[4,128,2560]{2,1,0:T(8,128)(2,1)S(1)} custom-call(bf16[64,2560]{1,0:T(8,128)(2,1)S(1)} %convolution_convert_fusion.state_ref, f32[4,2560]{1,0:T(4,128)S(1)} %reshape.172.reach_ref, bf16[128,64]{1,0:T(8,128)(2,1)S(1)} %slice.80.c_ref, f32[128,2560]{1,0:T(8,128)S(1)} %fusion.5.base_ref, f32[128,2560]{1,0:T(8,128)S(1)} %copy.86.fade_ref, ...), custom_call_target="tpu_custom_call" | custom-call | flops 1073741824 | bytes 67108864 | tf_op jit(solution)/shard_map/pallas_call | solution.py:415
  78.2 1.5 copy-done.1
  79.7 1.7 copy-done.2
  81.5 1.1 copy-done.4
  82.6 138.0 %shard_map.146 = bf16[128,2560]{1,0:T(8,128)(2,1)S(1)} custom-call(bf16[4,128,2560]{2,1,0:T(8,128)(2,1)S(1)} %copy-done.2, bf16[2560,640]{1,0:T(8,128)(2,1)} %all-gather.3.cloned.1.call-done.weight_hbm, bf16[128,2560]{1,0:T(8,128)(2,1)S(1)} %bitcast.68, f32[1,2560]{1,0:T(1,128)S(1)} %broadcast_in_dim.103.gain_ref, bf16[2560,512]{1,0:T(8,128)(2,1)} %bitcast.76, ...), custom_call_target="tpu_custom_call" | custom-call | flops 6442450944 | bytes 67108864 | tf_op jit(solution)/shard_map/pallas_call | solution.py:465
  220.6 0.8 copy.93
  (39 shorter events, 0.2 us)
Async XLA Ops:
  6.5 1.5 copy-start
  6.5 15.4 %copy-start.12 = (s32[1,128,2]{1,2,0:T(2,128)S(1)}, s32[1,128,2]{1,2,0:T(2,128)}, u32[]{:S(2)}) copy-start(s32[1,128,2]{1,2,0:T(2,128)} %param.28) | copy-start | bytes 3076
  6.5 9.0 %copy-start.9 = (f32[1,128,40]{1,2,0:T(8,128)S(1)}, f32[1,128,40]{1,2,0:T(8,128)}, u32[]{:S(2)}) copy-start(f32[1,128,40]{1,2,0:T(8,128)} %param.17) | copy-start | bytes 61444
  6.5 9.1 %copy-start.15 = (f32[40]{0:T(128)S(1)}, f32[40]{0:T(128)}, u32[]{:S(2)}) copy-start(f32[40]{0:T(128)} %param.18) | copy-start | bytes 484
  6.5 15.5 %copy-start.8 = (f32[4,2688]{1,0:T(4,128)S(1)}, f32[4,2688]{1,0:T(4,128)}, u32[]{:S(2)}) copy-start(f32[4,2688]{1,0:T(4,128)} %param.16) | copy-start | bytes 129028
  6.5 73.2 %all-gather.3.cloned.1.call-start = ((), (), s32[]{:S(2)}) async-start(), calls=%async_computation | async-start | bytes 3686400 | tf_op jit(solution)/shard_map/all_gather | solution.py:367
  8.8 16.2 %copy-start.14 = (f32[40]{0:T(128)S(1)}, f32[40]{0:T(128)}, u32[]{:S(2)}) copy-start(f32[40]{0:T(128)} %param.19) | copy-start | bytes 484
  10.2 20.7 %collective-permute-start = (bf16[3,2688]{1,0:T(4,128)(2,1)}, bf16[3,2688]{1,0:T(4,128)(2,1)}, u32[]{:S(2)}, u32[]{:S(2)}) collective-permute-start(bf16[3,2688]{1,0:T(4,128)(2,1)} %slice_bitcast_fusion), channel_id=1, source_target_pairs={{0,8},{8,16},{16,24},{1,9},{9,17},{17,25},{2,10},{10,18},{18,26},{... | collective-permute-start | bytes 48392 | tf_op jit(solution)/shard_map/ppermute | solution.py:16
  28.2 1.8 copy-start.11
  28.2 1.8 copy-start.13
  33.7 1.1 copy-start.5
  33.8 4.3 %copy-start.10 = (f32[40,128]{1,0:T(8,128)S(1)}, f32[40,128]{1,0:T(8,128)}, u32[]{:S(2)}) copy-start(f32[40,128]{1,0:T(8,128)} %copy.83) | copy-start | bytes 61444
  44.2 2.3 copy-start.6
  44.2 2.6 %copy-start.7 = (f32[128,2560]{1,0:T(8,128)S(1)}, f32[128,2560]{1,0:T(8,128)}, u32[]{:S(2)}) copy-start(f32[128,2560]{1,0:T(8,128)} %copy.84) | copy-start | bytes 3932164
  46.8 1.1 copy-start.3
  78.2 1.5 copy-start.1
  79.7 1.7 copy-start.2
  81.5 1.1 copy-start.4
Sparse Core Ops, SparseCore 0:
  13.3 63.9 all-gather.2

commit v4 on v3

--- a/solution.py
+++ b/solution.py
@@ -115,9 +115,9 @@
 def exchange_kernel(
     ring,
     experts,
-    rows_ref,
+    rows_hbm,
     weight_hbm,
-    residual_ref,
+    residual_hbm,
     gain_ref,
     gate_hbm,
     up_hbm,
@@ -128,6 +128,8 @@
     pair_ref,
     out_ref,
     weight_ref,
+    rows_ref,
+    residual_ref,
     gate_ref,
     up_ref,
     down_ref,
@@ -159,7 +161,14 @@
     locals_ = [
         pltpu.make_async_copy(source, target, local_sem.at[index])
         for index, (source, target) in enumerate(
-            ((weight_hbm, weight_ref), (gate_hbm, gate_ref), (up_hbm, up_ref), (down_hbm, down_ref))
+            (
+                (weight_hbm, weight_ref),
+                (rows_hbm, rows_ref),
+                (residual_hbm, residual_ref),
+                (gate_hbm, gate_ref),
+                (up_hbm, up_ref),
+                (down_hbm, down_ref),
+            )
         )
     ]
     for copy in locals_:
@@ -208,27 +217,42 @@
             device_id_type=pl.DeviceIdType.MESH,
         )
 
-    def out_copy(shift):
+    def out_copy(target, slot):
         return pltpu.make_async_remote_copy(
-            src_ref=outgoing.at[shift],
-            dst_ref=arrived.at[shift],
-            send_sem=out_send.at[shift],
-            recv_sem=out_recv.at[shift],
-            device_id={"grp": lax.rem(mine + shift, experts)},
+            src_ref=outgoing.at[target],
+            dst_ref=arrived.at[slot],
+            send_sem=out_send.at[target],
+            recv_sem=out_recv.at[slot],
+            device_id={"grp": target},
             device_id_type=pl.DeviceIdType.MESH,
         )
 
-    def back_copy(shift):
+    def back_copy(target, slot):
         return pltpu.make_async_remote_copy(
-            src_ref=result.at[shift],
-            dst_ref=returned.at[shift],
-            send_sem=back_send.at[shift],
-            recv_sem=back_recv.at[shift],
-            device_id={"grp": lax.rem(mine + experts - shift, experts)},
+            src_ref=result.at[target],
+            dst_ref=returned.at[slot],
+            send_sem=back_send.at[target],
+            recv_sem=back_recv.at[slot],
+            device_id={"grp": target},
             device_id_type=pl.DeviceIdType.MESH,
         )
 
+    pairs = experts // 2
+    other = lax.rem(mine + 1, experts)
+
+    def partner(step):
+        here = mine // 2
+        if pairs & (pairs - 1):
+            return lax.rem(here + step, pairs)
+        place = 0
+        bit = 1
+        while bit < pairs:
+            place = place + lax.rem(here // bit + step // bit, 2) * bit
+            bit *= 2
+        return place
+
     locals_[0].wait()
+    locals_[1].wait()
 
     def project(index, carry):
         slot = ring - 1 - index
@@ -244,6 +268,7 @@
 
     lax.fori_loop(0, ring, project, 0)
     share_in[me] = share_out[0]
+    locals_[2].wait()
 
     def mix(index, squares):
         @pl.when(index != me)
@@ -262,52 +287,63 @@
     scale = lax.rsqrt(squares * (1.0 / width) + EPSILON)
     moe_ref[...] = (mixed_ref[:, :width].astype(full) * scale * gain_ref[...]).astype(half)
 
-    def dispatch(shift, carry):
-        outgoing[shift] = jnp.dot(
-            send_pick_ref[shift], moe_ref[...], preferred_element_type=full
-        ).astype(half)
-
-        @pl.when(shift > 0)
-        def _():
-            out_copy(shift).start()
-
-        return carry
-
-    lax.fori_loop(1, experts, dispatch, 0)
-    arrived[0] = jnp.dot(send_pick_ref[0], moe_ref[...], preferred_element_type=full).astype(half)
-    for copy in locals_[1:]:
+    def dispatch(index, carry):
+        low = partner(pairs - 1 - index) * 2
+        outgoing[pl.ds(low, 2)] = (
+            jnp.dot(
+                send_pick_ref[pl.ds(low, 2)].reshape(2 * capacity, moe_ref.shape[0]),
+                moe_ref[...],
+                preferred_element_type=full,
+            )
+            .astype(half)
+            .reshape(2, capacity, width)
+        )
+        for target in (low, low + 1):
+
+            @pl.when(target != mine)
+            def _():
+                out_copy(target, mine).start()
+
+        return carry
+
+    lax.fori_loop(0, pairs, dispatch, 0)
+    arrived[mine] = outgoing[mine]
+    for copy in locals_[3:]:
         copy.wait()
 
-    def run_expert(pair, carry):
-        low = pair * 2
-
-        @pl.when(low > 0)
-        def _():
-            out_copy(low).wait_recv()
-
-        out_copy(low + 1).wait_recv()
+    def run_expert(step, carry):
+        low = partner(step) * 2
+        for origin in (low, low + 1):
+
+            @pl.when(origin != mine)
+            def _():
+                out_copy(other, origin).wait_recv()
+
         rows = arrived[pl.ds(low, 2)].reshape(2 * capacity, width)
         gate_part = jnp.dot(rows, gate_ref[...], preferred_element_type=full)
         up_part = jnp.dot(rows, up_ref[...], preferred_element_type=full)
         hidden = (gate_part * jax.nn.sigmoid(gate_part) * up_part).astype(half)
         made = jnp.dot(hidden, down_ref[...], preferred_element_type=full).astype(half)
         result[pl.ds(low, 2)] = made.reshape(2, capacity, width)
-
-        @pl.when(low > 0)
+        for origin in (low, low + 1):
+
+            @pl.when(origin != mine)
+            def _():
+                back_copy(origin, mine).start()
+
+        return carry
+
+    lax.fori_loop(0, pairs, run_expert, 0)
+    returned[mine] = result[mine]
+
+    def take_back(slot, carry):
+        @pl.when(slot != mine)
         def _():
-            back_copy(low).start()
-
-        back_copy(low + 1).start()
-        return carry
-
-    lax.fori_loop(0, experts // 2, run_expert, 0)
-    returned[0] = result[0]
-
-    def take_back(shift, carry):
-        back_copy(shift).wait_recv()
-        return carry
-
-    lax.fori_loop(1, experts, take_back, 0)
+            back_copy(other, slot).wait_recv()
+
+        return carry
+
+    lax.fori_loop(0, experts, take_back, 0)
     first_weight = pair_ref[:, 0:1]
     second_weight = pair_ref[:, 1:2]
 
@@ -329,13 +365,16 @@
         share_copy(shift).wait_send()
         return carry
 
-    def drain_grp(shift, carry):
-        out_copy(shift).wait_send()
-        back_copy(shift).wait_send()
+    def drain_grp(target, carry):
+        @pl.when(target != mine)
+        def _():
+            out_copy(target, mine).wait_send()
+            back_copy(target, mine).wait_send()
+
         return carry
 
     lax.fori_loop(1, ring, drain_seq, 0)
-    lax.fori_loop(1, experts, drain_grp, 0)
+    lax.fori_loop(0, experts, drain_grp, 0)
 
 
 def on_device(
@@ -444,7 +483,7 @@
     )
     experts = lax.axis_size("grp")
     capacity = 4 * row_count // experts
-    flat_picks = (routes[0].reshape(-1) - lax.axis_index("grp") + experts) % experts
+    flat_picks = routes[0].reshape(-1)
     member = (flat_picks[:, None] == jnp.arange(experts)[None, :]).astype(jnp.int32)
     position = jnp.cumsum(member, axis=0) - member
     slot_index = jnp.sum(position * member, axis=1)
@@ -465,10 +504,12 @@
     layer_out = pl.pallas_call(
         functools.partial(exchange_kernel, ring, experts),
         out_shape=jax.ShapeDtypeStruct((row_count, model_width), half),
-        in_specs=[vmem, anywhere, vmem, vmem, anywhere, anywhere, anywhere, vmem, vmem, vmem, vmem],
+        in_specs=[anywhere, anywhere, anywhere, vmem, anywhere, anywhere, anywhere, vmem, vmem, vmem, vmem],
         out_specs=vmem,
         scratch_shapes=[
             pltpu.VMEM((inner_width, share), half),
+            pltpu.VMEM((ring, row_count, inner_width), half),
+            pltpu.VMEM((row_count, ring * share), half),
             pltpu.VMEM((model_width, hidden_width), half),
             pltpu.VMEM((model_width, hidden_width), half),
             pltpu.VMEM((hidden_width, model_width), half),
@@ -480,7 +521,7 @@
             slab,
             slab,
             slab,
-            pltpu.SemaphoreType.DMA((4,)),
+            pltpu.SemaphoreType.DMA((6,)),
         ]
         + [pltpu.SemaphoreType.DMA((ring,))] * 2
         + [pltpu.SemaphoreType.DMA((experts,))] * 4,

time: 229 us -> 227 us (level)
  the two profiles are of different devices: /device:TPU:0 before, /device:TPU:28 now
where the time goes in v4:
time: 227 us; the launch traced here: 226 us
  Pallas kernels  167 us (74%)
  local copies, waits for them, and re-layouts  25.8 us (11%)
  between operations  13.7 us (6%)
  matrix products  6.61 us (3%)
  other arithmetic  5.14 us (2%)
  blocking collectives  5.04 us (2%)
  starting transfers between devices  2.49 us (1%)
    pallas_call x1, Pallas kernels, on_device(): pl.pallas_call(functools.partial(exchange_kernel, ring, experts), out_sha...  137 us
    pallas_call x1, Pallas kernels, on_device(): pl.pallas_call(functools.partial(mixer_kernel, ring // 2), out_shape=jax....  29.9 us
    unnamed x35, local copies, waits for them, and re-layouts  8.85 us
    all_gather x1, blocking collectives, on_device(): totals = lax.all_gather(cumulative[-1], 'seq', axis=0)  5.04 us
  transfers between devices with their start and end apart: 2, of which 0 were waited for; matrix products, arithmetic and copies ran while one was open for 12% of the time, Pallas kernels for 13%

profile of v4, /device:TPU:28, one launch (start us, length us, event | category | flops | bytes accessed | tf_op | source)
XLA Modules:
  0.0 225.9 jit_solution(8099068296719122246)
XLA Ops:
  6.5 0.0 all-gather.3.cloned.1.call-start
  6.6 1.4 copy-done
  8.0 0.8 constant_dynamic-slice_fusion
  8.8 1.4 slice_bitcast_fusion
  10.2 2.5 %collective-permute-start = (bf16[3,2688]{1,0:T(4,128)(2,1)}, bf16[3,2688]{1,0:T(4,128)(2,1)}, u32[]{:S(2)}, u32[]{:S(2)}) collective-permute-start(bf16[3,2688]{1,0:T(4,128)(2,1)} %slice_bitcast_fusion), channel_id=1, source_target_pairs={{0,8},{8,16},{16,24},{1,9},{9,17},{17,25},{2,10},{10,18},{18,26},{... | collective-permute-start | bytes 48392 | tf_op jit(solution)/shard_map/ppermute | solution.py:16
  12.6 0.0 all-gather.3.cloned.1.call-update
  12.6 0.8 copy.76
  13.4 0.1 eq.77
  13.6 0.1 eq.73
  13.7 0.6 reduce-window.6
  14.3 0.2 slice_reduce_fusion.6
  14.6 0.1 fusion.24
  14.7 0.1 reduce_sum.25
  14.8 0.1 reduce_sum.24
  15.0 0.1 copy.66
  15.1 0.1 copy.79
  15.2 0.1 negate_multiply_fusion
  15.2 0.2 reduce_window_sum.26
  15.4 5.0 %all-gather = f32[4,1,40]{2,1,0:T(1,128)S(1)} all-gather(f32[1,1,40]{2,1,0:T(1,128)S(1)} %get-tuple-element.18), channel_id=1, replica_groups=mesh['seq'=4,'grp'=8] {'seq'}, dimensions={0}, use_global_device_ids=true | all-gather | bytes 800 | tf_op jit(solution)/shard_map/all_gather | solution.py:445
  20.5 0.1 fusion.27
  20.6 0.1 select_reduce_fusion
  20.7 0.2 slice_reduce_fusion
  20.9 0.1 fusion.13
  20.9 0.0 copy-done.8
  20.9 0.7 slice_reduce_fusion.5
  21.7 0.1 exponential_select_fusion
  21.7 0.1 fusion.14
  21.8 0.1 fusion.37
  21.9 0.6 iota_compare_fusion.3
  22.5 0.7 copy.72
  23.2 0.7 copy.70
  23.9 0.1 broadcast_in_dim.99
  23.9 0.1 mul.134
  24.0 0.1 broadcast_in_dim.96
  24.1 0.1 reshape.145.reach_ref
  24.2 0.1 copy.67
  24.2 0.1 broadcast_in_dim.90
  24.4 1.5 copy.68
  25.8 0.1 copy.74
  25.9 1.2 broadcast_in_dim.100
  27.1 1.7 copy.75.fade_ref
  28.9 0.1 copy.80
  29.0 0.7 broadcast_in_dim.102.gain_ref
  29.7 0.0 collective-permute-done
  29.7 1.3 maximum_convert_fusion
  31.0 1.6 multiply_convert_fusion.1
  32.6 1.0 slice.78
  33.6 0.1 copy-done.5
  33.7 0.1 slice.80.c_ref
  33.7 2.2 copy.69
  35.9 1.0 fusion.20
  36.9 0.0 copy-done.10
  36.9 3.3 %fusion.3 = f32[40,64,128]{2,1,0:T(8,128)} fusion(bf16[128,40,64]{0,2,1:T(8,128)(2,1)} %bitcast.69, f32[40,128]{1,0:T(8,128)S(1)} %copy-done.10, f32[40,128]{1,0:T(8,128)} %copy.70, f32[128,128]{1,0:T(8,128)S(1)} %fusion.20, pred[128,128]{1,0:T(8,128)(4,1)} %iota_compare_fusion.3), kind=kOutput, calls=%fused_computation.12 | convolution fusion | flops 87818240 | bytes 2088960 | tf_op jit(solution)/shard_map/hts,shp->thp/dot_general | solution.py:451
  40.3 2.8 %copy.73 = f32[128,2560]{1,0:T(8,128)} copy(f32[128,2560]{0,1:T(8,128)} %bitcast.67) | data formatting | bytes 2621440 | tf_op jit(solution)/shard_map/reshape | solution.py:452
  43.1 2.3 %convolution_convert_fusion.state_ref = bf16[64,2560]{1,0:T(8,128)(2,1)S(1)} fusion(f32[128,2560]{1,0:T(8,128)} %copy.68, bf16[128,2688]{1,0:T(8,128)(2,1)} %copy-done.5), kind=kOutput, calls=%fused_computation | convolution fusion | flops 43089920 | bytes 2326528 | tf_op jit(solution)/shard_map/dot_general | solution.py:439
  45.4 0.2 copy-done.7
  45.6 0.2 fusion.5.base_ref
  45.8 0.9 copy-done.3
  46.7 29.9 %shard_map.145.rows_hbm = bf16[4,128,2560]{2,1,0:T(8,128)(2,1)S(1)} custom-call(bf16[64,2560]{1,0:T(8,128)(2,1)S(1)} %convolution_convert_fusion.state_ref, f32[4,2560]{1,0:T(4,128)S(1)} %reshape.145.reach_ref, bf16[128,64]{1,0:T(8,128)(2,1)S(1)} %slice.80.c_ref, f32[128,2560]{1,0:T(8,128)S(1)} %fusion.5.base_ref, f32[128,2560]{1,0:T(8,128)S(1)} %copy.75.fade_ref, ...), custom_call_target="tpu_custom_call" | custom-call | flops 1073741824 | bytes 67108864 | tf_op jit(solution)/shard_map/pallas_call | solution.py:454
  76.6 1.5 copy-done.1
  78.1 1.7 copy-done.2
  79.8 1.1 copy-done.4
  80.9 137.3 %shard_map.146 = bf16[128,2560]{1,0:T(8,128)(2,1)S(1)} custom-call(bf16[4,128,2560]{2,1,0:T(8,128)(2,1)S(1)} %copy-done.2, bf16[2560,640]{1,0:T(8,128)(2,1)} %all-gather.3.cloned.1.call-done.weight_hbm, bf16[128,2560]{1,0:T(8,128)(2,1)S(1)} %bitcast.64, f32[1,2560]{1,0:T(1,128)S(1)} %broadcast_in_dim.102.gain_ref, bf16[2560,512]{1,0:T(8,128)(2,1)} %bitcast.72, ...), custom_call_target="tpu_custom_call" | custom-call | flops 6442450944 | bytes 67108864 | tf_op jit(solution)/shard_map/pallas_call | solution.py:504
  218.2 0.8 copy.82
  (33 shorter events, 0.2 us)
Async XLA Ops:
  6.5 1.4 copy-start
  6.5 8.4 %copy-start.9 = (f32[1,128,40]{1,2,0:T(8,128)S(1)}, f32[1,128,40]{1,2,0:T(8,128)}, u32[]{:S(2)}) copy-start(f32[1,128,40]{1,2,0:T(8,128)} %param.17) | copy-start | bytes 61444
  6.5 8.5 %copy-start.14 = (f32[40]{0:T(128)S(1)}, f32[40]{0:T(128)}, u32[]{:S(2)}) copy-start(f32[40]{0:T(128)} %param.18) | copy-start | bytes 484
  6.5 14.4 %copy-start.8 = (f32[4,2688]{1,0:T(4,128)S(1)}, f32[4,2688]{1,0:T(4,128)}, u32[]{:S(2)}) copy-start(f32[4,2688]{1,0:T(4,128)} %param.16) | copy-start | bytes 129028
  6.5 71.5 %all-gather.3.cloned.1.call-start = ((), (), s32[]{:S(2)}) async-start(), calls=%async_computation | async-start | bytes 3686400 | tf_op jit(solution)/shard_map/all_gather | solution.py:406
  10.2 13.7 %copy-start.13 = (f32[40]{0:T(128)S(1)}, f32[40]{0:T(128)}, u32[]{:S(2)}) copy-start(f32[40]{0:T(128)} %param.19) | copy-start | bytes 484
  10.2 19.6 %collective-permute-start = (bf16[3,2688]{1,0:T(4,128)(2,1)}, bf16[3,2688]{1,0:T(4,128)(2,1)}, u32[]{:S(2)}, u32[]{:S(2)}) collective-permute-start(bf16[3,2688]{1,0:T(4,128)(2,1)} %slice_bitcast_fusion), channel_id=1, source_target_pairs={{0,8},{8,16},{16,24},{1,9},{9,17},{17,25},{2,10},{10,18},{18,26},{... | collective-permute-start | bytes 48392 | tf_op jit(solution)/shard_map/ppermute | solution.py:16
  27.1 1.8 copy-start.11
  27.1 1.8 copy-start.12
  32.6 1.1 copy-start.5
  32.6 4.3 %copy-start.10 = (f32[40,128]{1,0:T(8,128)S(1)}, f32[40,128]{1,0:T(8,128)}, u32[]{:S(2)}) copy-start(f32[40,128]{1,0:T(8,128)} %copy.72) | copy-start | bytes 61444
  43.1 2.3 %copy-start.6 = (bf16[128,2688]{1,0:T(8,128)(2,1)S(1)}, bf16[128,2688]{1,0:T(8,128)(2,1)}, u32[]{:S(2)}) copy-start(bf16[128,2688]{1,0:T(8,128)(2,1)} %copy-done.5) | copy-start | bytes 2064388
  43.1 2.5 %copy-start.7 = (f32[128,2560]{1,0:T(8,128)S(1)}, f32[128,2560]{1,0:T(8,128)}, u32[]{:S(2)}) copy-start(f32[128,2560]{1,0:T(8,128)} %copy.73) | copy-start | bytes 3932164
  45.6 1.1 copy-start.3
  76.6 1.5 copy-start.1
  78.1 1.7 copy-start.2
  79.8 1.1 copy-start.4
Sparse Core Ops, SparseCore 0:
  12.8 60.4 all-gather.2

commit v5 on v4

--- a/solution.py
+++ b/solution.py
@@ -141,6 +141,10 @@
     arrived,
     result,
     returned,
+    hub_rows,
+    hub_pick,
+    hub_send,
+    hub_recv,
     local_sem,
     share_send,
     share_recv,
@@ -217,15 +221,35 @@
             device_id_type=pl.DeviceIdType.MESH,
         )
 
-    def out_copy(target, slot):
+    side = experts // 2
+    hub = lax.rem(mine + side, experts)
+
+    def out_copy(buffer, target, slot):
         return pltpu.make_async_remote_copy(
-            src_ref=outgoing.at[target],
+            src_ref=outgoing.at[buffer],
             dst_ref=arrived.at[slot],
-            send_sem=out_send.at[target],
+            send_sem=out_send.at[buffer],
             recv_sem=out_recv.at[slot],
             device_id={"grp": target},
             device_id_type=pl.DeviceIdType.MESH,
         )
+
+    hub_copies = [
+        pltpu.make_async_remote_copy(
+            src_ref=source_ref,
+            dst_ref=target_ref,
+            send_sem=hub_send.at[index],
+            recv_sem=hub_recv.at[index],
+            device_id={"grp": hub},
+            device_id_type=pl.DeviceIdType.MESH,
+        )
+        for index, (source_ref, target_ref) in enumerate(
+            (
+                (moe_ref, hub_rows),
+                (send_pick_ref.at[pl.ds(hub // side * side, side)], hub_pick),
+            )
+        )
+    ]
 
     def back_copy(target, slot):
         return pltpu.make_async_remote_copy(
@@ -287,27 +311,47 @@
     scale = lax.rsqrt(squares * (1.0 / width) + EPSILON)
     moe_ref[...] = (mixed_ref[:, :width].astype(full) * scale * gain_ref[...]).astype(half)
 
-    def dispatch(index, carry):
-        low = partner(pairs - 1 - index) * 2
+    for copy in hub_copies:
+        copy.start()
+
+    def fill(low, picks, rows):
         outgoing[pl.ds(low, 2)] = (
             jnp.dot(
-                send_pick_ref[pl.ds(low, 2)].reshape(2 * capacity, moe_ref.shape[0]),
-                moe_ref[...],
-                preferred_element_type=full,
+                picks.reshape(2 * capacity, moe_ref.shape[0]), rows, preferred_element_type=full
             )
             .astype(half)
             .reshape(2, capacity, width)
         )
+
+    def dispatch(index, carry):
+        low = partner(pairs // 2 - 1 - index) * 2
+        fill(low, send_pick_ref[pl.ds(low, 2)], moe_ref[...])
         for target in (low, low + 1):
 
             @pl.when(target != mine)
             def _():
-                out_copy(target, mine).start()
-
-        return carry
-
-    lax.fori_loop(0, pairs, dispatch, 0)
+                out_copy(target, target, mine).start()
+
+        return carry
+
+    def forward(index, carry):
+        low = partner(pairs // 2 - 1 - index) * 2
+        buffer = lax.rem(low + side, experts)
+        fill(buffer, hub_pick[pl.ds(lax.rem(low, side), 2)], hub_rows[...])
+        for turn in range(2):
+
+            @pl.when(low + turn != mine)
+            def _():
+                out_copy(buffer + turn, low + turn, hub).start()
+
+        return carry
+
+    lax.fori_loop(0, pairs // 2, dispatch, 0)
     arrived[mine] = outgoing[mine]
+    for copy in hub_copies:
+        copy.wait_recv()
+    lax.fori_loop(0, pairs // 2, forward, 0)
+    arrived[hub] = outgoing[hub]
     for copy in locals_[3:]:
         copy.wait()
 
@@ -315,9 +359,9 @@
         low = partner(step) * 2
         for origin in (low, low + 1):
 
-            @pl.when(origin != mine)
+            @pl.when((origin != mine) & (origin != hub))
             def _():
-                out_copy(other, origin).wait_recv()
+                out_copy(other, other, origin).wait_recv()
 
         rows = arrived[pl.ds(low, 2)].reshape(2 * capacity, width)
         gate_part = jnp.dot(rows, gate_ref[...], preferred_element_type=full)
@@ -368,13 +412,18 @@
     def drain_grp(target, carry):
         @pl.when(target != mine)
         def _():
-            out_copy(target, mine).wait_send()
             back_copy(target, mine).wait_send()
+
+        @pl.when((target != mine) & (target != hub))
+        def _():
+            out_copy(target, other, mine).wait_send()
 
         return carry
 
     lax.fori_loop(1, ring, drain_seq, 0)
     lax.fori_loop(0, experts, drain_grp, 0)
+    for copy in hub_copies:
+        copy.wait_send()
 
 
 def on_device(
@@ -521,6 +570,10 @@
             slab,
             slab,
             slab,
+            whole_rows,
+            pltpu.VMEM((experts // 2, capacity, row_count), half),
+            pltpu.SemaphoreType.DMA((2,)),
+            pltpu.SemaphoreType.DMA((2,)),
             pltpu.SemaphoreType.DMA((6,)),
         ]
         + [pltpu.SemaphoreType.DMA((ring,))] * 2

time: 227 us -> 201 us (0.89)
  the two profiles are of different devices: /device:TPU:28 before, /device:TPU:0 now
where the time goes in v5:
time: 201 us; the launch traced here: 198 us
  Pallas kernels  138 us (69%)
  local copies, waits for them, and re-layouts  25.8 us (13%)
  between operations  13.7 us (7%)
  matrix products  6.59 us (3%)
  blocking collectives  5.7 us (3%)
  other arithmetic  5.13 us (3%)
  starting transfers between devices  3.11 us (2%)
    pallas_call x1, Pallas kernels, on_device(): pl.pallas_call(functools.partial(exchange_kernel, ring, experts), out_sha...  107 us
    pallas_call x1, Pallas kernels, on_device(): pl.pallas_call(functools.partial(mixer_kernel, ring // 2), out_shape=jax....  30.4 us
    unnamed x35, local copies, waits for them, and re-layouts  8.87 us
    all_gather x1, blocking collectives, on_device(): totals = lax.all_gather(cumulative[-1], 'seq', axis=0)  5.7 us
  transfers between devices with their start and end apart: 2, of which 0 were waited for; matrix products, arithmetic and copies ran while one was open for 14% of the time, Pallas kernels for 15%

profile of v5, /device:TPU:0, one launch (start us, length us, event | category | flops | bytes accessed | tf_op | source)
XLA Modules:
  0.0 197.7 jit_solution(848723768778128317)
XLA Ops:
  6.5 0.0 all-gather.3.cloned.1.call-start
  6.6 1.4 copy-done
  8.0 0.8 constant_dynamic-slice_fusion
  8.8 1.4 slice_bitcast_fusion
  10.2 3.1 %collective-permute-start = (bf16[3,2688]{1,0:T(4,128)(2,1)}, bf16[3,2688]{1,0:T(4,128)(2,1)}, u32[]{:S(2)}, u32[]{:S(2)}) collective-permute-start(bf16[3,2688]{1,0:T(4,128)(2,1)} %slice_bitcast_fusion), channel_id=1, source_target_pairs={{0,8},{8,16},{16,24},{1,9},{9,17},{17,25},{2,10},{10,18},{18,26},{... | collective-permute-start | bytes 48392 | tf_op jit(solution)/shard_map/ppermute | solution.py:16
  13.2 0.0 all-gather.3.cloned.1.call-update
  13.3 0.8 copy.76
  14.1 0.1 eq.77
  14.2 0.1 eq.73
  14.3 0.6 reduce-window.6
  14.9 0.2 slice_reduce_fusion.6
  15.2 0.1 fusion.24
  15.3 0.1 reduce_sum.25
  15.4 0.1 reduce_sum.24
  15.6 0.1 copy.66
  15.7 0.0 copy-done.14
  15.7 0.1 copy.79
  15.9 0.2 reduce_window_sum.26
  16.0 5.7 %all-gather = f32[4,1,40]{2,1,0:T(1,128)S(1)} all-gather(f32[1,1,40]{2,1,0:T(1,128)S(1)} %get-tuple-element.18), channel_id=1, replica_groups=mesh['seq'=4,'grp'=8] {'seq'}, dimensions={0}, use_global_device_ids=true | all-gather | bytes 800 | tf_op jit(solution)/shard_map/all_gather | solution.py:494
  21.8 0.1 fusion.27
  21.9 0.1 select_reduce_fusion
  22.0 0.2 slice_reduce_fusion
  22.1 0.1 fusion.13
  22.2 0.7 slice_reduce_fusion.5
  22.9 0.1 exponential_select_fusion
  23.0 0.1 fusion.14
  23.1 0.1 fusion.37
  23.2 0.6 iota_compare_fusion.3
  23.8 0.7 copy.72
  24.5 0.7 copy.70
  25.1 0.1 broadcast_in_dim.99
  25.2 0.1 mul.134
  25.3 0.1 broadcast_in_dim.96
  25.4 0.1 reshape.145.reach_ref
  25.5 0.1 copy.67
  25.5 0.1 broadcast_in_dim.90
  25.6 1.5 copy.68
  27.1 0.1 copy.74
  27.2 1.2 broadcast_in_dim.100
  28.4 1.7 copy.75.fade_ref
  30.2 0.0 copy-done.12
  30.2 0.1 copy.80
  30.3 0.7 broadcast_in_dim.102.gain_ref
  31.0 0.0 collective-permute-done
  31.0 1.3 maximum_convert_fusion
  32.3 1.6 multiply_convert_fusion.1
  33.9 1.0 slice.78
  34.9 0.1 copy-done.5
  34.9 0.1 slice.80.c_ref
  35.0 2.2 %copy.69 = bf16[128,2560]{0,1:T(8,128)(2,1)} copy(bf16[128,2560]{1,0:T(8,128)(2,1)} %slice.78) | data formatting | bytes 1310720 | tf_op jit(solution)/shard_map/slice | solution.py:472
  37.2 1.0 fusion.20
  38.2 0.0 copy-done.10
  38.2 3.3 %fusion.3 = f32[40,64,128]{2,1,0:T(8,128)} fusion(bf16[128,40,64]{0,2,1:T(8,128)(2,1)} %bitcast.69, f32[40,128]{1,0:T(8,128)S(1)} %copy-done.10, f32[40,128]{1,0:T(8,128)} %copy.70, f32[128,128]{1,0:T(8,128)S(1)} %fusion.20, pred[128,128]{1,0:T(8,128)(4,1)} %iota_compare_fusion.3), kind=kOutput, calls=%fused_computation.12 | convolution fusion | flops 87818240 | bytes 2088960 | tf_op jit(solution)/shard_map/hts,shp->thp/dot_general | solution.py:500
  41.5 2.8 %copy.73 = f32[128,2560]{1,0:T(8,128)} copy(f32[128,2560]{0,1:T(8,128)} %bitcast.67) | data formatting | bytes 2621440 | tf_op jit(solution)/shard_map/reshape | solution.py:501
  44.4 2.3 %convolution_convert_fusion.state_ref = bf16[64,2560]{1,0:T(8,128)(2,1)S(1)} fusion(f32[128,2560]{1,0:T(8,128)} %copy.68, bf16[128,2688]{1,0:T(8,128)(2,1)} %copy-done.5), kind=kOutput, calls=%fused_computation | convolution fusion | flops 43089920 | bytes 2326528 | tf_op jit(solution)/shard_map/dot_general | solution.py:488
  46.6 0.3 copy-done.7
  46.9 0.2 fusion.5.base_ref
  47.1 0.9 copy-done.3
  48.0 30.4 %shard_map.145.rows_hbm = bf16[4,128,2560]{2,1,0:T(8,128)(2,1)S(1)} custom-call(bf16[64,2560]{1,0:T(8,128)(2,1)S(1)} %convolution_convert_fusion.state_ref, f32[4,2560]{1,0:T(4,128)S(1)} %reshape.145.reach_ref, bf16[128,64]{1,0:T(8,128)(2,1)S(1)} %slice.80.c_ref, f32[128,2560]{1,0:T(8,128)S(1)} %fusion.5.base_ref, f32[128,2560]{1,0:T(8,128)S(1)} %copy.75.fade_ref, ...), custom_call_target="tpu_custom_call" | custom-call | flops 1073741824 | bytes 67108864 | tf_op jit(solution)/shard_map/pallas_call | solution.py:503
  78.4 1.5 copy-done.1
  79.9 1.7 copy-done.2
  81.6 1.1 copy-done.4
  82.7 107.3 %shard_map.146 = bf16[128,2560]{1,0:T(8,128)(2,1)S(1)} custom-call(bf16[4,128,2560]{2,1,0:T(8,128)(2,1)S(1)} %copy-done.2, bf16[2560,640]{1,0:T(8,128)(2,1)} %all-gather.3.cloned.1.call-done.weight_hbm, bf16[128,2560]{1,0:T(8,128)(2,1)S(1)} %bitcast.64, f32[1,2560]{1,0:T(1,128)S(1)} %broadcast_in_dim.102.gain_ref, bf16[2560,512]{1,0:T(8,128)(2,1)} %bitcast.72, ...), custom_call_target="tpu_custom_call" | custom-call | flops 6442450944 | bytes 67108864 | tf_op jit(solution)/shard_map/pallas_call | solution.py:553
  190.0 0.8 copy.82
  (33 shorter events, 0.2 us)
Async XLA Ops:
  6.5 1.4 copy-start
  6.5 9.0 %copy-start.9 = (f32[1,128,40]{1,2,0:T(8,128)S(1)}, f32[1,128,40]{1,2,0:T(8,128)}, u32[]{:S(2)}) copy-start(f32[1,128,40]{1,2,0:T(8,128)} %param.17) | copy-start | bytes 61444
  6.5 9.1 %copy-start.14 = (f32[40]{0:T(128)S(1)}, f32[40]{0:T(128)}, u32[]{:S(2)}) copy-start(f32[40]{0:T(128)} %param.18) | copy-start | bytes 484
  6.5 15.7 %copy-start.8 = (f32[4,2688]{1,0:T(4,128)S(1)}, f32[4,2688]{1,0:T(4,128)}, u32[]{:S(2)}) copy-start(f32[4,2688]{1,0:T(4,128)} %param.16) | copy-start | bytes 129028
  6.5 73.3 %all-gather.3.cloned.1.call-start = ((), (), s32[]{:S(2)}) async-start(), calls=%async_computation | async-start | bytes 3686400 | tf_op jit(solution)/shard_map/all_gather | solution.py:455
  10.2 15.0 %copy-start.13 = (f32[40]{0:T(128)S(1)}, f32[40]{0:T(128)}, u32[]{:S(2)}) copy-start(f32[40]{0:T(128)} %param.19) | copy-start | bytes 484
  10.2 20.9 %collective-permute-start = (bf16[3,2688]{1,0:T(4,128)(2,1)}, bf16[3,2688]{1,0:T(4,128)(2,1)}, u32[]{:S(2)}, u32[]{:S(2)}) collective-permute-start(bf16[3,2688]{1,0:T(4,128)(2,1)} %slice_bitcast_fusion), channel_id=1, source_target_pairs={{0,8},{8,16},{16,24},{1,9},{9,17},{17,25},{2,10},{10,18},{18,26},{... | collective-permute-start | bytes 48392 | tf_op jit(solution)/shard_map/ppermute | solution.py:16
  28.4 1.8 copy-start.11
  28.4 1.8 copy-start.12
  33.9 1.1 copy-start.5
  33.9 4.3 %copy-start.10 = (f32[40,128]{1,0:T(8,128)S(1)}, f32[40,128]{1,0:T(8,128)}, u32[]{:S(2)}) copy-start(f32[40,128]{1,0:T(8,128)} %copy.72) | copy-start | bytes 61444
  44.3 2.3 %copy-start.6 = (bf16[128,2688]{1,0:T(8,128)(2,1)S(1)}, bf16[128,2688]{1,0:T(8,128)(2,1)}, u32[]{:S(2)}) copy-start(bf16[128,2688]{1,0:T(8,128)(2,1)} %copy-done.5) | copy-start | bytes 2064388
  44.3 2.6 %copy-start.7 = (f32[128,2560]{1,0:T(8,128)S(1)}, f32[128,2560]{1,0:T(8,128)}, u32[]{:S(2)}) copy-start(f32[128,2560]{1,0:T(8,128)} %copy.73) | copy-start | bytes 3932164
  46.9 1.1 copy-start.3
  78.3 1.5 copy-start.1
  79.9 1.7 copy-start.2
  81.6 1.1 copy-start.4
Sparse Core Ops, SparseCore 0:
  13.4 63.9 all-gather.2
